TPU v7x, 256 devices: a whole 4x4x8 slice. The times are simulated.
256 devices in a mesh: seq: 64 (over z, y, core), head: 2 (over x_lo), sample: 2 (over x_hi).
Axes of the slice: x: 4 (x_hi: 2, x_lo: 2; x = x_hi * 2 + x_lo), y: 4, z: 8, core: 2. Of those that a mesh axis runs over, the one named last changes fastest.
Arguments:
- features: bfloat16 [2, 16384, 1536], P('sample', 'seq'), may hold values from -16 to 16
- dilated_weight: bfloat16 [1536, 3, 768], P(None, None, 'head'), may hold values from -0.09375 to 0.09375
- point_weight: bfloat16 [1536, 768], P(None, 'head'), may hold values from -0.21875 to 0.21875
- track_weight: bfloat16 [1536, 3840], P('sample', 'head'), may hold values from -0.15625 to 0.15625
- track_cotangent: bfloat16 [2, 16384, 3840], P('sample', 'seq', 'head'), may hold values from -6 to 6
Outputs:
- input_grad: bfloat16 [2, 16384, 1536], P('sample', 'seq')
- dilated_grad: float32 [1536, 3, 768], P(('seq', 'sample'), None, 'head')
- point_grad: float32 [1536, 768], P(('seq', 'sample'), 'head')
All inputs are finite; a program needn't handle non-finite values.
Results may differ from a plain program's by a relative error of at most 0.015.
Values may be sent and summed in bfloat16 or wider, within the bound.
A program may use at most 128 MiB of HBM per device.

v0:
```python
import jax
import jax.numpy as jnp
from jax import lax
from jax.sharding import Mesh
from jax.sharding import PartitionSpec as P

DIST = 4
SEQ = ("seq_0", "seq_1", "seq_2")
SEQ_SAMPLE = ("seq_0", "seq_1", "seq_2", "sample")


def passed_along(value, axis, steps):
    count = lax.axis_size(axis)
    leading, last = (max(0, -steps), min(count, count - steps))
    return lax.ppermute(value, axis, [(source, source + steps) for source in range(leading, last)])


def from_everyone(value, axis):
    size = lax.axis_size(axis)
    return lax.all_to_all(
        jnp.broadcast_to(value[None], (size, *value.shape)), axis, 0, 0, tiled=True
    )


def over_copies(value, axis):
    return from_everyone(value, axis).astype(jnp.float32).sum(axis=0)


def sum_by_axis(subtotal, axes):
    for axis in axes:
        subtotal = lax.psum_scatter(subtotal, axis, scatter_dimension=0, tiled=True)
    return subtotal


def cut_along(value, dim, size):
    shape = value.shape
    tiles = value.reshape(*shape[:dim], size, shape[dim] // size, *shape[dim + 1 :])
    return jnp.moveaxis(tiles, dim, 0)


def sent_and_summed(value, axis, dim):
    tiles = cut_along(value, dim, lax.axis_size(axis))
    arrived = lax.all_to_all(tiles, axis, split_axis=0, concat_axis=0, tiled=True)
    return arrived.astype(jnp.float32).sum(axis=0)


def gelu_value(value):
    inner = 0.7978845608 * (value + 0.044715 * value * value * value)
    return 0.5 * value * (1.0 + jnp.tanh(inner))


def gelu_slope(value):
    inner = 0.7978845608 * (value + 0.044715 * value * value * value)
    tangent = jnp.tanh(inner)
    return 0.5 * (1.0 + tangent) + 0.5 * value * (1.0 - tangent * tangent) * 0.7978845608 * (
        1.0 + 3.0 * 0.044715 * value * value
    )


def times_transposed(left, right):
    return lax.dot_general(
        left, right, (((1,), (1,)), ((), ())), preferred_element_type=jnp.float32
    )


def transposed_times(left, right):
    return lax.dot_general(
        left, right, (((0,), (0,)), ((), ())), preferred_element_type=jnp.float32
    )


def shift_inputs(field, amount):
    return passed_along(field, SEQ, amount)


def shift_grads(field, amount):
    return passed_along(field, SEQ, amount)


def pair_sum(term):
    return over_copies(term.astype(jnp.bfloat16), "head").astype(jnp.float32)


def body(features, dilated_weight, point_weight, track_weight, track_cotangent):
    samples, positions, channels = features.shape
    number_rows = samples * positions
    group_width = dilated_weight.shape[2]
    feat_wide = features.reshape(number_rows, channels).astype(jnp.float32)
    activated_hidden = gelu_value(feat_wide).astype(jnp.bfloat16)
    flat_weight = dilated_weight.reshape(channels, 3 * group_width)
    preceding_value = shift_inputs(activated_hidden, DIST)
    following_value = shift_inputs(activated_hidden, -DIST)
    middle = jnp.dot(preceding_value, dilated_weight[:, 0, :], preferred_element_type=jnp.float32)
    middle = middle + jnp.dot(
        activated_hidden, dilated_weight[:, 1, :], preferred_element_type=jnp.float32
    )
    middle = middle + jnp.dot(
        following_value, dilated_weight[:, 2, :], preferred_element_type=jnp.float32
    )
    hidden = gelu_value(middle).astype(jnp.bfloat16)
    block_out = (feat_wide + pair_sum(times_transposed(hidden, point_weight))).astype(jnp.bfloat16)
    whole_track = lax.all_gather(track_weight, "sample", axis=0, tiled=True)
    scores = jnp.dot(block_out, whole_track, preferred_element_type=jnp.float32)
    cotangent = track_cotangent.reshape(number_rows, whole_track.shape[1])
    score_grad = (cotangent.astype(jnp.float32) * jax.nn.sigmoid(scores)).astype(jnp.bfloat16)
    out_grad = pair_sum(times_transposed(score_grad, whole_track))
    out_grad_b = out_grad.astype(jnp.bfloat16)
    hidden_grad = jnp.dot(out_grad_b, point_weight, preferred_element_type=jnp.float32)
    middle_gradient = (hidden_grad * gelu_slope(middle)).astype(jnp.bfloat16)
    later = shift_grads(middle_gradient, -DIST)
    earlier = shift_grads(middle_gradient, DIST)
    kernel_taps = jnp.concatenate([later, middle_gradient, earlier], axis=1)
    act_grad = pair_sum(times_transposed(kernel_taps, flat_weight))
    input_grad = (out_grad + act_grad * gelu_slope(feat_wide)).astype(jnp.bfloat16)
    partial_value = sum_by_axis(
        jnp.concatenate(
            [transposed_times(activated_hidden, kernel_taps), transposed_times(out_grad_b, hidden)],
            axis=1,
        ),
        SEQ,
    )
    summed = sent_and_summed(partial_value.astype(jnp.bfloat16), "sample", 0)
    dilated_grad = summed[:, : 3 * group_width].reshape(summed.shape[0], 3, group_width)
    point_grad = summed[:, 3 * group_width :]
    return (input_grad.reshape(samples, positions, channels), dilated_grad, point_grad)


def solution(mesh):
    torus = Mesh(
        mesh.devices.reshape(8, 4, 2, mesh.shape["head"], mesh.shape["sample"]),
        ("seq_0", "seq_1", "seq_2", "head", "sample"),
    )
    placed = (
        P("sample", SEQ, None),
        P(None, None, "head"),
        P(None, "head"),
        P("sample", "head"),
        P("sample", SEQ, "head"),
    )
    return jax.shard_map(
        body,
        mesh=torus,
        in_specs=placed,
        out_specs=(P("sample", SEQ, None), P(SEQ_SAMPLE, None, "head"), P(SEQ_SAMPLE, "head")),
        check_vma=False,
    )
```

profile of v0, /device:TPU:1, one launch (start us, length us, event | category | flops | bytes accessed | tf_op | source)
XLA Modules:
  0.0 349.5 jit_solution(3809542777656043403)
XLA Ops:
  9.0 1.6 collective-permute-start.1
  10.5 6.3 %collective-permute-start = (bf16[256,1536]{1,0:T(8,128)(2,1)S(1)}, bf16[256,1536]{1,0:T(8,128)(2,1)S(1)}, u32[]{:S(2)}, u32[]{:S(2)}) collective-permute-start(bf16[256,1536]{1,0:T(8,128)(2,1)S(1)} %fusion.21), channel_id=1, source_target_pairs={{0,16},{4,20},{8,24},{12,28},{16,32},{20,36},{24,40},{28,44},{32,4... | collective-permute-start | bytes 2359304 | tf_op jit(solution)/shard_map/ppermute | solution.py:15
  16.9 2.0 fusion.32
  18.9 11.2 %collective-permute-done.1 = bf16[256,1536]{1,0:T(8,128)(2,1)S(1)} collective-permute-done((bf16[256,1536]{1,0:T(8,128)(2,1)S(1)}, bf16[256,1536]{1,0:T(8,128)(2,1)S(1)}, u32[]{:S(2)}, u32[]{:S(2)}) %collective-permute-start.1) | collective-permute-done | bytes 786464 | tf_op jit(solution)/shard_map/ppermute | solution.py:15
  30.6 19.2 %collective-permute-done = bf16[256,1536]{1,0:T(8,128)(2,1)S(1)} collective-permute-done((bf16[256,1536]{1,0:T(8,128)(2,1)S(1)}, bf16[256,1536]{1,0:T(8,128)(2,1)S(1)}, u32[]{:S(2)}, u32[]{:S(2)}) %collective-permute-start) | collective-permute-done | bytes 786464 | tf_op jit(solution)/shard_map/ppermute | solution.py:15
  51.2 39.1 %all_to_all.20 = bf16[2,256,1536]{2,1,0:T(8,128)(2,1)S(1)} all-to-all(bf16[2,256,1536]{2,1,0:T(8,128)(2,1)S(1)} %broadcast_in_dim.6), channel_id=1, replica_groups=mesh['seq_0'=8,'seq_1'=4,'seq_2'=2,'head'=2,'sample'=2] {'head'}, dimensions={0} | all-to-all | bytes 3145728 | tf_op jit(solution)/shard_map/all_to_all | solution.py:20
  90.3 1.4 convert_reduce_fusion.2
  91.7 21.1 %all-gather.2.cloned.1.call-done = bf16[1536,1920]{1,0:T(8,128)(2,1)} async-done(((bf16[768,1920]{1,0:T(8,128)(2,1)}), bf16[1536,1920]{1,0:T(8,128)(2,1)}) %all-gather.2.cloned.1.call-update) | async-done | bytes 5898256 | tf_op jit(solution)/shard_map/all_gather | solution.py:102
  112.8 9.4 %convolution_convert_fusion = bf16[256,1536]{1,0:T(8,128)(2,1)} fusion(bf16[1536,1920]{1,0:T(8,128)(2,1)} %all-gather.2.cloned.1.call-done, bf16[1,256,1920]{2,1,0:T(8,128)(2,1)} %param.9, f32[256,1536]{1,0:T(8,128)} %convert_reduce_fusion.2, bf16[1,256,1536]{2,1,0:T(8,128)(2,1)S(1)} %copy-done.2), kind=kOutput, calls=%fused_computation.24 | convolution fusion | flops 3024420864 | bytes 10027008 | tf_op jit(solution)/shard_map/dot_general | solution.py:61
  122.3 1.2 broadcast_in_dim.7
  123.5 21.0 %all_to_all.21 = bf16[2,256,1536]{2,1,0:T(8,128)(2,1)S(1)} all-to-all(bf16[2,256,1536]{2,1,0:T(8,128)(2,1)S(1)} %broadcast_in_dim.7), channel_id=1, replica_groups=mesh['seq_0'=8,'seq_1'=4,'seq_2'=2,'head'=2,'sample'=2] {'head'}, dimensions={0} | all-to-all | bytes 3145728 | tf_op jit(solution)/shard_map/all_to_all | solution.py:20
  145.4 4.8 %collective-permute-start.3 = (bf16[256,384]{1,0:T(8,128)(2,1)S(1)}, bf16[256,384]{1,0:T(8,128)(2,1)S(1)}, u32[]{:S(2)}, u32[]{:S(2)}) collective-permute-start(bf16[256,384]{1,0:T(8,128)(2,1)S(1)} %fusion.38), channel_id=1, source_target_pairs={{0,16},{4,20},{8,24},{12,28},{16,32},{20,36},{24,40},{28,44},{32,4... | collective-permute-start | bytes 589832 | tf_op jit(solution)/shard_map/ppermute | solution.py:15
  150.2 1.3 collective-permute-start.2
  151.5 1.5 fusion.52
  153.1 5.1 %collective-permute-done.2 = bf16[256,384]{1,0:T(8,128)(2,1)S(1)} collective-permute-done((bf16[256,384]{1,0:T(8,128)(2,1)S(1)}, bf16[256,384]{1,0:T(8,128)(2,1)S(1)}, u32[]{:S(2)}, u32[]{:S(2)}) %collective-permute-start.2) | collective-permute-done | bytes 196640 | tf_op jit(solution)/shard_map/ppermute | solution.py:15
  158.2 4.1 %fusion.55 = f32[1536,1152]{0,1:T(8,128)} fusion(bf16[256,384]{1,0:T(8,128)(2,1)S(1)} %collective-permute-done.3, bf16[256,384]{1,0:T(8,128)(2,1)S(1)} %fusion.38, bf16[256,384]{1,0:T(8,128)(2,1)S(1)} %collective-permute-done.2, bf16[1,256,1536]{2,1,0:T(8,128)(2,1)S(1)} %copy-done.3), kind=kOutput, calls=%fused_computation.74 | convolution fusion | flops 911671296 | bytes 8454144 | tf_op jit(solution)/shard_map/dot_general | solution.py:67
  162.2 7.8 %pad_maximum_fusion = f32[1536,1536]{0,1:T(8,128)} fusion(f32[1536,384]{0,1:T(8,128)S(1)} %fusion.52, f32[1536,1152]{0,1:T(8,128)} %fusion.55), kind=kLoop, calls=%fused_computation | loop fusion | flops 2359296 | bytes 18874368 | tf_op jit(solution)/shard_map/concatenate | solution.py:116
  170.0 9.6 %copy.16 = f32[1536,1536]{1,0:T(8,128)} copy(f32[1536,1536]{0,1:T(8,128)} %pad_maximum_fusion) | data formatting | bytes 18874368
  179.8 106.6 %reduce-scatter.10.cloned.1.call-done = f32[192,1536]{1,0:T(8,128)} async-done(((f32[1536,1536]{1,0:T(8,128)}), f32[192,1536]{1,0:T(8,128)}) %reduce-scatter.10.cloned.1.call-update) | async-done | bytes 1179664
  286.5 6.1 %copy.14 = bf16[1536,3,384]{0,2,1:T(8,128)(2,1)} copy(bf16[1536,3,384]{2,0,1:T(8,128)(2,1)} %param.6) | data formatting | bytes 7077888 | tf_op args[1]
  292.6 3.2 convolution_convert_fusion.2
  295.8 1.3 broadcast_in_dim.8
  297.1 4.6 %all-to-all-start.2 = ((bf16[2,256,1536]{2,1,0:T(8,128)(2,1)}), bf16[2,256,1536]{2,1,0:T(8,128)(2,1)}, u32[]{:S(2)}, u32[]{:S(2)}) async-start(bf16[2,256,1536]{2,1,0:T(8,128)(2,1)} %broadcast_in_dim.8), calls=%async_computation.2 | async-start | bytes 3145728 | tf_op jit(solution)/shard_map/all_to_all | solution.py:20
  301.7 11.2 %reduce-scatter.12.cloned.1.call-done = f32[48,1536]{1,0:T(8,128)} async-done(((f32[192,1536]{1,0:T(8,128)}), f32[48,1536]{1,0:T(8,128)}) %reduce-scatter.12.cloned.1.call-update) | async-done | bytes 294928
  313.0 7.4 %all-to-all-done.2 = bf16[2,256,1536]{2,1,0:T(8,128)(2,1)} async-done(((bf16[2,256,1536]{2,1,0:T(8,128)(2,1)}), bf16[2,256,1536]{2,1,0:T(8,128)(2,1)}, u32[]{:S(2)}, u32[]{:S(2)}) %all-to-all-start.2) | async-done | bytes 1572896 | tf_op jit(solution)/shard_map/all_to_all | solution.py:20
  320.4 3.0 convert_reduce_fusion
  323.3 7.2 %reduce-scatter.14.cloned.1.call-done = f32[24,1536]{1,0:T(8,128)} async-done(((f32[48,1536]{1,0:T(8,128)}), f32[24,1536]{1,0:T(8,128)}) %reduce-scatter.14.cloned.1.call-update) | async-done | bytes 147472 | tf_op jit(solution)/shard_map/reduce_scatter | solution.py:31
  330.5 0.9 convert_element_type.87
  332.1 4.0 %all-to-all-start.3 = ((bf16[2,12,1536]{2,1,0:T(8,128)(2,1)}), bf16[2,12,1536]{2,1,0:T(8,128)(2,1)}, u32[]{:S(2)}, u32[]{:S(2)}) async-start(bf16[2,12,1536]{2,1,0:T(8,128)(2,1)} %reshape.29), calls=%async_computation.3 | async-start | bytes 196608 | tf_op jit(solution)/shard_map/all_to_all | solution.py:43
  336.1 3.5 fusion.19
  339.5 1.2 all-to-all-done.3
  340.8 0.9 convert_reduce_fusion.3
  (42 shorter events, 6.8 us)
Async XLA Ops:
  7.2 43.3 %copy-start = (bf16[1536,384]{1,0:T(8,128)(2,1)S(1)}, bf16[1536,384]{1,0:T(8,128)(2,1)}, u32[]{:S(2)}) copy-start(bf16[1536,384]{1,0:T(8,128)(2,1)} %param.7) | copy-start | bytes 3538948
  7.2 1.2 copy-start.2
  7.2 105.6 %all-gather.2.cloned.1.call-start = ((), (), s32[]{:S(2)}) async-start(), calls=%async_computation.7 | async-start | bytes 8847360 | tf_op jit(solution)/shard_map/all_gather | solution.py:102
  7.9 278.5 %reduce-scatter.10.cloned.1.call-start = ((), (), s32[]{:S(2)}) async-start(), calls=%async_computation.8 | async-start | bytes 10616832
  9.0 21.1 %copy-start.5 = (bf16[1536,3,384]{2,0,1:T(8,128)(2,1)S(1)}, bf16[1536,3,384]{2,0,1:T(8,128)(2,1)}, u32[]{:S(2)}) copy-start(bf16[1536,3,384]{2,0,1:T(8,128)(2,1)} %param.6) | copy-start | bytes 10616836
  9.0 21.1 %collective-permute-start.1 = (bf16[256,1536]{1,0:T(8,128)(2,1)S(1)}, bf16[256,1536]{1,0:T(8,128)(2,1)S(1)}, u32[]{:S(2)}, u32[]{:S(2)}) collective-permute-start(bf16[256,1536]{1,0:T(8,128)(2,1)S(1)} %fusion.21), channel_id=1, source_target_pairs={{16,0},{20,4},{24,8},{28,12},{32,16},{36,20},{40,24},{44,28},{48,3... | collective-permute-start | bytes 2359304 | tf_op jit(solution)/shard_map/ppermute | solution.py:15
  10.5 39.3 %collective-permute-start = (bf16[256,1536]{1,0:T(8,128)(2,1)S(1)}, bf16[256,1536]{1,0:T(8,128)(2,1)S(1)}, u32[]{:S(2)}, u32[]{:S(2)}) collective-permute-start(bf16[256,1536]{1,0:T(8,128)(2,1)S(1)} %fusion.21), channel_id=1, source_target_pairs={{0,16},{4,20},{8,24},{12,28},{16,32},{20,36},{24,40},{28,44},{32,4... | collective-permute-start | bytes 2359304 | tf_op jit(solution)/shard_map/ppermute | solution.py:15
  50.5 94.3 %copy-start.6 = (f32[256,384]{1,0:T(8,128)}, f32[256,384]{1,0:T(8,128)S(1)}, u32[]{:S(2)}) copy-start(f32[256,384]{1,0:T(8,128)S(1)} %fusion.29) | copy-start | bytes 1179652
  145.4 12.7 %copy-start.7 = (bf16[256,384]{1,0:T(8,128)(2,1)}, bf16[256,384]{1,0:T(8,128)(2,1)S(1)}, u32[]{:S(2)}) copy-start(bf16[256,384]{1,0:T(8,128)(2,1)S(1)} %fusion.38) | copy-start | bytes 589828
  145.4 12.7 %copy-start.3 = (bf16[1,256,1536]{2,1,0:T(8,128)(2,1)S(1)}, bf16[1,256,1536]{2,1,0:T(8,128)(2,1)}, u32[]{:S(2)}) copy-start(bf16[1,256,1536]{2,1,0:T(8,128)(2,1)} %param.5) | copy-start | bytes 2359300
  145.4 7.6 %collective-permute-start.3 = (bf16[256,384]{1,0:T(8,128)(2,1)S(1)}, bf16[256,384]{1,0:T(8,128)(2,1)S(1)}, u32[]{:S(2)}, u32[]{:S(2)}) collective-permute-start(bf16[256,384]{1,0:T(8,128)(2,1)S(1)} %fusion.38), channel_id=1, source_target_pairs={{0,16},{4,20},{8,24},{12,28},{16,32},{20,36},{24,40},{28,44},{32,4... | collective-permute-start | bytes 589832 | tf_op jit(solution)/shard_map/ppermute | solution.py:15
  150.2 7.9 %collective-permute-start.2 = (bf16[256,384]{1,0:T(8,128)(2,1)S(1)}, bf16[256,384]{1,0:T(8,128)(2,1)S(1)}, u32[]{:S(2)}, u32[]{:S(2)}) collective-permute-start(bf16[256,384]{1,0:T(8,128)(2,1)S(1)} %fusion.38), channel_id=1, source_target_pairs={{16,0},{20,4},{24,8},{28,12},{32,16},{36,20},{40,24},{44,28},{48,3... | collective-permute-start | bytes 589832 | tf_op jit(solution)/shard_map/ppermute | solution.py:15
  158.2 4.1 %copy-start.9 = (bf16[256,384]{1,0:T(8,128)(2,1)}, bf16[256,384]{1,0:T(8,128)(2,1)S(1)}, u32[]{:S(2)}) copy-start(bf16[256,384]{1,0:T(8,128)(2,1)S(1)} %collective-permute-done.2) | copy-start | bytes 589828
  179.6 133.3 %reduce-scatter.12.cloned.1.call-start = ((), (), s32[]{:S(2)}) async-start(), calls=%async_computation.9 | async-start | bytes 1474560
  286.5 6.1 %copy-start.8 = (bf16[256,384]{1,0:T(8,128)(2,1)S(1)}, bf16[256,384]{1,0:T(8,128)(2,1)}, u32[]{:S(2)}) copy-start(bf16[256,384]{1,0:T(8,128)(2,1)} %copy-done.7) | copy-start | bytes 589828
  286.5 6.1 %copy-start.10 = (bf16[256,384]{1,0:T(8,128)(2,1)S(1)}, bf16[256,384]{1,0:T(8,128)(2,1)}, u32[]{:S(2)}) copy-start(bf16[256,384]{1,0:T(8,128)(2,1)} %copy-done.9) | copy-start | bytes 589828
  297.1 23.3 %all-to-all-start.2 = ((bf16[2,256,1536]{2,1,0:T(8,128)(2,1)}), bf16[2,256,1536]{2,1,0:T(8,128)(2,1)}, u32[]{:S(2)}, u32[]{:S(2)}) async-start(bf16[2,256,1536]{2,1,0:T(8,128)(2,1)} %broadcast_in_dim.8), calls=%async_computation.2 | async-start | bytes 3145728 | tf_op jit(solution)/shard_map/all_to_all | solution.py:20
  301.7 28.8 %reduce-scatter.14.cloned.1.call-start = ((), (), s32[]{:S(2)}) async-start(), calls=%async_computation.10 | async-start | bytes 442368 | tf_op jit(solution)/shard_map/reduce_scatter | solution.py:31
  313.0 23.1 %copy-start.4 = (bf16[1,256,1536]{2,1,0:T(8,128)(2,1)S(1)}, bf16[1,256,1536]{2,1,0:T(8,128)(2,1)}, u32[]{:S(2)}) copy-start(bf16[1,256,1536]{2,1,0:T(8,128)(2,1)} %param.5) | copy-start | bytes 2359300
  332.1 8.7 %all-to-all-start.3 = ((bf16[2,12,1536]{2,1,0:T(8,128)(2,1)}), bf16[2,12,1536]{2,1,0:T(8,128)(2,1)}, u32[]{:S(2)}, u32[]{:S(2)}) async-start(bf16[2,12,1536]{2,1,0:T(8,128)(2,1)} %reshape.29), calls=%async_computation.3 | async-start | bytes 196608 | tf_op jit(solution)/shard_map/all_to_all | solution.py:43
  336.0 6.9 %copy-start.1 = (bf16[1536,384]{1,0:T(8,128)(2,1)S(1)}, bf16[1536,384]{1,0:T(8,128)(2,1)}, u32[]{:S(2)}) copy-start(bf16[1536,384]{1,0:T(8,128)(2,1)} %param.7) | copy-start | bytes 3538948
Sparse Core Ops, SparseCore 0:
  9.8 102.9 all-gather.1
  179.7 106.6 reduce-scatter.9
  289.0 23.8 reduce-scatter.11
  315.3 15.1 reduce-scatter.13
where the time goes:
time: 350 us
  waiting for transfers between devices  191 us (55%)
  blocking collectives  60 us (17%)
  starting transfers between devices  22.9 us (7%)
  matrix products  22.7 us (6%)
  local copies, waits for them, and re-layouts  20.7 us (6%)
  other arithmetic  18.3 us (5%)
  between operations  14 us (4%)
    unnamed x6, waiting for transfers between devices  119 us
    all_to_all x2, blocking collectives, from_everyone(): lax.all_to_all(jnp.broadcast_to(value[None], (size, *value.shape)), axis,...  60 us
    ppermute x4, waiting for transfers between devices, passed_along(): lax.ppermute(value, axis, [(source, source + steps) for source in range(l...  35.5 us
    all_gather x1, waiting for transfers between devices, body(): whole_track = lax.all_gather(track_weight, 'sample', axis=0, tiled=True)  21.1 us
    unnamed x24, local copies, waits for them, and re-layouts  16.2 us
    ppermute x4, starting transfers between devices, passed_along(): lax.ppermute(value, axis, [(source, source + steps) for source in range(l...  13.9 us
    dot_general x3, matrix products, times_transposed(): lax.dot_general(left, right, (((1,), (1,)), ((), ())), preferred_element_...  13.2 us
    concatenate x1, other arithmetic, body(): jnp.concatenate([transposed_times(activated_hidden, kernel_taps), transpo...  7.77 us
  transfers between devices with their start and end apart: 10, of which 9 were waited for; matrix products, arithmetic and copies ran while one was open for 7% of the time, Pallas kernels for 0%

commit v1 on v0

v1 whole, which is shorter than its diff:
```python
import jax
import jax.numpy as jnp
from jax import lax
from jax.experimental import pallas as pl
from jax.experimental.pallas import tpu as pltpu
from jax.sharding import Mesh
from jax.sharding import PartitionSpec as P

MESH = pl.DeviceIdType.MESH
SEQ = ("z", "y", "c")
SEQ_SAMPLE = ("z", "y", "c", "s")
NZ, NY = 8, 4
YROWS, ZROWS = 64, 16
SUBS = 4
VMEM = pl.BlockSpec(memory_space=pltpu.VMEM)
ANY = pl.BlockSpec(memory_space=pl.ANY)
DMA = pltpu.SemaphoreType.DMA


def gelu_value(value):
    inner = 0.7978845608 * (value + 0.044715 * value * value * value)
    return 0.5 * value * (1.0 + jnp.tanh(inner))


def gelu_slope(value):
    inner = 0.7978845608 * (value + 0.044715 * value * value * value)
    tangent = jnp.tanh(inner)
    return 0.5 * (1.0 + tangent) + 0.5 * value * (1.0 - tangent * tangent) * 0.7978845608 * (
        1.0 + 3.0 * 0.044715 * value * value
    )


def times(left, right):
    return jnp.dot(left, right, preferred_element_type=jnp.float32)


def times_transposed(left, right):
    return lax.dot_general(
        left, right, (((1,), (1,)), ((), ())), preferred_element_type=jnp.float32
    )


def transposed_times(left, right):
    return lax.dot_general(
        left, right, (((0,), (0,)), ((), ())), preferred_element_type=jnp.float32
    )


def place():
    return tuple(lax.axis_index(name) for name in ("z", "y", "c", "h", "s"))


def remote(source, target, sent, arrived, **device):
    return pltpu.make_async_remote_copy(
        src_ref=source,
        dst_ref=target,
        send_sem=sent,
        recv_sem=arrived,
        device_id=device,
        device_id_type=MESH,
    )


def greet(barrier, **device):
    pl.semaphore_signal(barrier, inc=1, device_id=device, device_id_type=MESH)


def rows_at(start, size):
    return pl.ds(pl.multiple_of(start, 16), size)


def shifted(z, y, step):
    at = z * NY + y + step
    return {"z": lax.div(at, NY), "y": lax.rem(at, NY)}


def has_neighbours(z, y):
    at = z * NY + y
    return at >= 2, at < NZ * NY - 2


def send_halo(z, y, ahead, behind, sent, arrived):
    before, after = has_neighbours(z, y)

    @pl.when(after)
    def _():
        remote(*ahead, sent.at[0], arrived.at[0], **shifted(z, y, 2)).start()

    @pl.when(before)
    def _():
        remote(*behind, sent.at[1], arrived.at[1], **shifted(z, y, -2)).start()


def wait_halo(z, y, ahead, behind, sent, arrived):
    before, after = has_neighbours(z, y)

    @pl.when(before)
    def _():
        remote(*ahead, sent.at[0], arrived.at[0], c=lax.axis_index("c")).wait_recv()

    @pl.when(jnp.logical_not(before))
    def _():
        ahead[1][...] = jnp.zeros_like(ahead[1])

    @pl.when(after)
    def _():
        remote(*behind, sent.at[1], arrived.at[1], c=lax.axis_index("c")).wait_recv()

    @pl.when(jnp.logical_not(after))
    def _():
        behind[1][...] = jnp.zeros_like(behind[1])


def drain_halo(z, y, ahead, behind, sent, arrived):
    before, after = has_neighbours(z, y)

    @pl.when(after)
    def _():
        remote(*ahead, sent.at[0], arrived.at[0], c=lax.axis_index("c")).wait_send()

    @pl.when(before)
    def _():
        remote(*behind, sent.at[1], arrived.at[1], c=lax.axis_index("c")).wait_send()


def greet_halo(barrier, z, y):
    before, after = has_neighbours(z, y)

    @pl.when(after)
    def _():
        greet(barrier, **shifted(z, y, 2))

    @pl.when(before)
    def _():
        greet(barrier, **shifted(z, y, -2))

    return before.astype(jnp.int32) + after.astype(jnp.int32)


def forward_kernel(
    q0, q2, centre, tw, pw, middle, hidden, twf, pwo,
    from_before, from_after, own, own_sem,
    halo_s, halo_r, hid_s, hid_r, x_s, x_r, y_s, y_r, tz_s, tz_r, pz_s, pz_r, sib_s, sib_r,
):
    z, y, c, h, s = place()
    up, down = lax.rem(z + 1, NZ), lax.rem(z + NZ - 1, NZ)
    barrier = pltpu.get_barrier_semaphore()
    greet(barrier, h=1 - h)
    greet(barrier, s=1 - s)
    greet(barrier, c=1 - c)
    greet(barrier, z=up)
    greet(barrier, z=down)
    for step in range(1, NY):
        greet(barrier, y=lax.rem(y + step, NY))
    count = greet_halo(barrier, z, y)
    pl.semaphore_wait(barrier, 8 + count)

    half = tw.shape[0] // 2
    pw_rows = pw.shape[0] // 2 // NZ
    base = c * half

    def y_piece(at):
        return rows_at(base + at * YROWS, YROWS)

    def z_piece(at):
        return rows_at(base + NY * YROWS + at * ZROWS, ZROWS)

    def p_piece(at):
        return rows_at(c * (pw.shape[0] // 2) + at * pw_rows, pw_rows)

    ahead, behind = (q0, from_before), (q2, from_after)
    send_halo(z, y, ahead, behind, halo_s, halo_r)
    to_sample = [
        remote(tw.at[z_piece(z)], twf.at[s, z_piece(z)], x_s.at[0], x_r.at[0], s=1 - s),
        remote(tw.at[y_piece(y)], twf.at[s, y_piece(y)], x_s.at[1], x_r.at[1], s=1 - s),
    ]
    to_head = remote(pw.at[p_piece(z)], pwo.at[p_piece(z)], x_s.at[2], x_r.at[2], h=1 - h)
    to_sample[0].start()
    to_head.start()
    to_sample[1].start()
    take_own = pltpu.make_async_copy(tw, own, own_sem.at[0])
    take_own.start()

    started = [*to_sample, to_head]
    landed = []
    other = 1 - s

    def track_sibling(rows, slot):
        copy = remote(twf.at[other, rows], twf.at[other, rows], sib_s.at[slot], sib_r.at[slot], c=1 - c)
        copy.start()
        started.append(copy)

    def point_sibling(rows, slot):
        copy = remote(pwo.at[rows], pwo.at[rows], sib_s.at[slot], sib_r.at[slot], c=1 - c)
        copy.start()
        started.append(copy)

    def send_z(at, slot, target):
        rows = z_piece(at)
        copy = remote(twf.at[other, rows], twf.at[other, rows], tz_s.at[slot], tz_r.at[slot], z=target)
        copy.start()
        started.append(copy)

    def send_p(at, slot, target):
        rows = p_piece(at)
        copy = remote(pwo.at[rows], pwo.at[rows], pz_s.at[slot], pz_r.at[slot], z=target)
        copy.start()
        started.append(copy)

    to_sample[0].wait_recv()
    send_z(z, 0, up)
    send_z(z, 4, down)
    to_head.wait_recv()
    send_p(z, 0, up)
    send_p(z, 4, down)
    track_sibling(z_piece(z), 0)
    point_sibling(p_piece(z), 8)

    take_own.wait()
    put_own = pltpu.make_async_copy(own, twf.at[s], own_sem.at[1])
    put_own.start()

    def ring_step(step):
        for send, sem_s, sem_r, buf, piece, slot, sibling, first in (
            (send_z, tz_s, tz_r, None, z_piece, 0, track_sibling, 0),
            (send_p, pz_s, pz_r, pwo, p_piece, 0, point_sibling, 8),
        ):
            ref = twf.at[other] if buf is None else buf
            at = lax.rem(z + NZ - step, NZ)
            remote(ref.at[piece(at)], ref.at[piece(at)], sem_s.at[step - 1], sem_r.at[step - 1], z=up).wait_recv()
            if step < 4:
                send(at, step, up)
            sibling(piece(at), first + step)
            if step < 4:
                at = lax.rem(z + step, NZ)
                remote(ref.at[piece(at)], ref.at[piece(at)], sem_s.at[step + 3], sem_r.at[step + 3], z=up).wait_recv()
                if step < 3:
                    send(at, 4 + step, down)
                sibling(piece(at), first + 4 + step)

    ring_step(1)
    to_sample[1].wait_recv()
    rows = y_piece(y)
    for step in range(1, NY):
        copy = remote(
            twf.at[other, rows], twf.at[other, rows], y_s.at[step - 1], y_r.at[step - 1],
            y=lax.rem(y + step, NY),
        )
        copy.start()
        started.append(copy)
    track_sibling(rows, 16)
    ring_step(2)

    wait_halo(z, y, ahead, behind, halo_s, halo_r)
    total = centre[...] + from_before[...].astype(jnp.float32) + from_after[...].astype(jnp.float32)
    middle[...] = total
    hidden[0] = gelu_value(total).astype(jnp.bfloat16)
    to_partner = remote(hidden.at[0], hidden.at[1], hid_s, hid_r, h=1 - h)
    to_partner.start()
    started.append(to_partner)
    ring_step(3)
    ring_step(4)
    for step in range(1, NY):
        rows = y_piece(lax.rem(y + NY - step, NY))
        remote(
            twf.at[other, rows], twf.at[other, rows], y_s.at[step - 1], y_r.at[step - 1], y=y
        ).wait_recv()
        track_sibling(rows, 16 + step)
    to_partner.wait_recv()

    sib_base = (1 - c) * half
    sib_point = (1 - c) * (pw.shape[0] // 2)
    for slot in range(20):
        step = slot % 8 if slot < 16 else slot - 16
        if slot < 16:
            at = lax.rem(z + NZ - step, NZ) if step <= 4 else lax.rem(z + step - 4, NZ)
        else:
            at = lax.rem(y + NY - step, NY)
        if slot < 8:
            ref = twf.at[other, rows_at(sib_base + NY * YROWS + at * ZROWS, ZROWS)]
        elif slot < 16:
            ref = pwo.at[rows_at(sib_point + at * pw_rows, pw_rows)]
        else:
            ref = twf.at[other, rows_at(sib_base + at * YROWS, YROWS)]
        remote(ref, ref, sib_s.at[slot], sib_r.at[slot], c=1 - c).wait_recv()
    for copy in started:
        copy.wait_send()
    drain_halo(z, y, ahead, behind, halo_s, halo_r)
    put_own.wait()


def forward_exchange(q0, q2, centre, tw, pw):
    rows, width = q0.shape
    return pl.pallas_call(
        forward_kernel,
        out_shape=(
            jax.ShapeDtypeStruct((rows, width), jnp.float32),
            jax.ShapeDtypeStruct((2, rows, width), jnp.bfloat16),
            jax.ShapeDtypeStruct((2, *tw.shape), jnp.bfloat16),
            jax.ShapeDtypeStruct(pw.shape, jnp.bfloat16),
        ),
        in_specs=[VMEM, VMEM, VMEM, ANY, ANY],
        out_specs=(VMEM, VMEM, ANY, ANY),
        scratch_shapes=[
            pltpu.VMEM((rows, width), jnp.bfloat16),
            pltpu.VMEM((rows, width), jnp.bfloat16),
            pltpu.VMEM(tw.shape, jnp.bfloat16),
            DMA((2,)),
            DMA((2,)), DMA((2,)),
            DMA, DMA,
            DMA((3,)), DMA((3,)),
            DMA((3,)), DMA((3,)),
            DMA((7,)), DMA((7,)),
            DMA((7,)), DMA((7,)),
            DMA((20,)), DMA((20,)),
        ],
        compiler_params=pltpu.CompilerParams(collective_id=0, has_side_effects=True),
        name="forward_exchange",
    )(q0, q2, centre, tw, pw)


def swap_kernel(mine, theirs, sent, arrived):
    h = lax.axis_index("h")
    barrier = pltpu.get_barrier_semaphore()
    greet(barrier, h=1 - h)
    pl.semaphore_wait(barrier, 1)
    copy = remote(mine, theirs, sent, arrived, h=1 - h)
    copy.start()
    copy.wait()


def head_swap(mine):
    return pl.pallas_call(
        swap_kernel,
        out_shape=jax.ShapeDtypeStruct(mine.shape, mine.dtype),
        in_specs=[VMEM],
        out_specs=VMEM,
        scratch_shapes=[DMA, DMA],
        compiler_params=pltpu.CompilerParams(collective_id=1, has_side_effects=True),
        name="head_swap",
    )(mine)


def halo_kernel(grad, later, earlier, sent, arrived):
    z, y, c, h, s = place()
    barrier = pltpu.get_barrier_semaphore()
    count = greet_halo(barrier, z, y)
    pl.semaphore_wait(barrier, count)
    ahead, behind = (grad, earlier), (grad, later)
    send_halo(z, y, ahead, behind, sent, arrived)
    wait_halo(z, y, ahead, behind, sent, arrived)
    drain_halo(z, y, ahead, behind, sent, arrived)


def halo_exchange(grad):
    shape = jax.ShapeDtypeStruct(grad.shape, grad.dtype)
    return pl.pallas_call(
        halo_kernel,
        out_shape=(shape, shape),
        in_specs=[VMEM],
        out_specs=(VMEM, VMEM),
        scratch_shapes=[DMA((2,)), DMA((2,))],
        compiler_params=pltpu.CompilerParams(collective_id=2, has_side_effects=True),
        name="halo_exchange",
    )(grad)


def reduce_kernel(
    grads, act, summed, act_other,
    sibling, sendbuf, recvbuf, final, last_send, last_recv,
    act_s, act_r, sib_s, sib_r, ring_s, ring_r, last_s, last_r,
):
    z, y, c, h, s = place()
    up, down = lax.rem(z + 1, NZ), lax.rem(z + NZ - 1, NZ)
    me = (y * 2 + c) * 2 + s

    def group(at):
        return {"y": lax.div(at, 4), "c": lax.rem(lax.div(at, 2), 2), "s": lax.rem(at, 2)}

    barrier = pltpu.get_barrier_semaphore()
    greet(barrier, c=1 - c)
    greet(barrier, z=up)
    greet(barrier, z=down)
    greet(barrier, h=1 - h)
    for step in range(1, 16):
        greet(barrier, **group(lax.rem(me + step, 16)))
    pl.semaphore_wait(barrier, 19)

    rows = grads.shape[1] // NZ
    width = grads.shape[2] // 2
    sub = rows // SUBS
    act_copy = remote(act, act_other, act_s, act_r, h=1 - h)
    order = (7, 1, 6, 2, 5, 3, 4, 0)
    siblings = []
    for slot, offset in enumerate(order):
        at = rows_at(lax.rem(z + offset, NZ) * rows, rows)
        copy = remote(grads.at[1 - c, at], sibling.at[at], sib_s.at[slot], sib_r.at[slot], c=1 - c)
        copy.start()
        siblings.append(copy)
    act_copy.start()

    def columns(way):
        return pl.ds(way * width, width)

    def partial(at, way, piece):
        where = rows_at(at * rows + piece * sub, sub)
        mine = grads[c, where, columns(way)].astype(jnp.float32)
        return mine + sibling[where, columns(way)].astype(jnp.float32)

    def ring_copy(step, way, piece):
        return remote(
            sendbuf.at[step, way, piece], recvbuf.at[step, way, piece],
            ring_s.at[step, way, piece], ring_r.at[step, way, piece], z=up if way == 0 else down,
        )

    def target(step, way):
        return lax.rem(z + 2 * NZ - 1 - step, NZ) if way == 0 else lax.rem(z + 1 + step, NZ)

    def ring_step(step):
        for piece in range(SUBS):
            for way in range(2):
                value = partial(target(step, way), way, piece)
                ring_copy(step - 1, way, piece).wait_recv()
                value = value + recvbuf[step - 1, way, piece].astype(jnp.float32)
                sendbuf[step, way, piece] = value.astype(jnp.bfloat16)
                ring_copy(step, way, piece).start()

    siblings[0].wait_recv()
    siblings[1].wait_recv()
    for piece in range(SUBS):
        for way in range(2):
            sendbuf[0, way, piece] = partial(target(0, way), way, piece).astype(jnp.bfloat16)
            ring_copy(0, way, piece).start()
    for copy in siblings[2:]:
        copy.wait_recv()

    def body(step, carry):
        ring_step(step)
        return carry

    lax.fori_loop(1, NZ - 1, body, 0)
    for piece in range(SUBS):
        for way in range(2):
            value = partial(z, way, piece)
            ring_copy(NZ - 2, way, piece).wait_recv()
            value = value + recvbuf[NZ - 2, way, piece].astype(jnp.float32)
            final[pl.ds(piece * sub, sub), columns(way)] = value
    each = rows // 16
    for at in range(16):
        last_send[at] = final[at * each:(at + 1) * each, :].astype(jnp.bfloat16)
    lasts = []
    for step in range(1, 16):
        to = lax.rem(me + step, 16)
        copy = remote(
            last_send.at[to], last_recv.at[me], last_s.at[step - 1], last_r.at[step - 1], **group(to)
        )
        copy.start()
        lasts.append(copy)
    last_recv[me] = last_send[me]
    for step in range(1, 16):
        source = lax.rem(me + 16 - step, 16)
        remote(
            last_send.at[source], last_recv.at[source], last_s.at[step - 1], last_r.at[step - 1], c=c
        ).wait_recv()
    for core in range(2):
        total = jnp.zeros((each, 2 * width), jnp.float32)
        for row in range(NY):
            for sample in range(2):
                total = total + last_recv[(row * 2 + core) * 2 + sample].astype(jnp.float32)
        summed[core] = total
    act_copy.wait()
    for copy in siblings:
        copy.wait_send()
    for copy in lasts:
        copy.wait_send()

    def drain(step, carry):
        for piece in range(SUBS):
            for way in range(2):
                ring_copy(step, way, piece).wait_send()
        return carry

    lax.fori_loop(0, NZ - 1, drain, 0)


def reduce_and_swap(grads, act):
    _, channels, width = grads.shape
    rows = channels // NZ
    each = rows // 16
    sub = rows // SUBS
    return pl.pallas_call(
        reduce_kernel,
        out_shape=(
            jax.ShapeDtypeStruct((2, each, width), jnp.float32),
            jax.ShapeDtypeStruct(act.shape, act.dtype),
        ),
        in_specs=[VMEM, VMEM],
        out_specs=(VMEM, VMEM),
        scratch_shapes=[
            pltpu.VMEM((channels, width), jnp.bfloat16),
            pltpu.VMEM((NZ - 1, 2, SUBS, sub, width // 2), jnp.bfloat16),
            pltpu.VMEM((NZ - 1, 2, SUBS, sub, width // 2), jnp.bfloat16),
            pltpu.VMEM((rows, width), jnp.float32),
            pltpu.VMEM((16, each, width), jnp.bfloat16),
            pltpu.VMEM((16, each, width), jnp.bfloat16),
            DMA, DMA,
            DMA((8,)), DMA((8,)),
            DMA((NZ - 1, 2, SUBS)), DMA((NZ - 1, 2, SUBS)),
            DMA((15,)), DMA((15,)),
        ],
        compiler_params=pltpu.CompilerParams(collective_id=3, has_side_effects=True),
        name="reduce_and_swap",
    )(grads, act)


def body(features, dilated_weight, point_weight, track_weight, track_cotangent):
    samples, positions, channels = features.shape
    number_rows = samples * positions
    width = dilated_weight.shape[2]
    feat_wide = features.reshape(number_rows, channels).astype(jnp.float32)
    activated = gelu_value(feat_wide).astype(jnp.bfloat16)
    taps_weight = [dilated_weight[:, tap, :] for tap in range(3)]
    to_later = times(activated, taps_weight[0]).astype(jnp.bfloat16)
    to_earlier = times(activated, taps_weight[2]).astype(jnp.bfloat16)
    centre = times(activated, taps_weight[1])
    middle, hidden, whole_track, other_point = forward_exchange(
        to_later, to_earlier, centre, track_weight, point_weight
    )
    whole_track = whole_track.reshape(channels, track_weight.shape[1])
    block_out = (
        feat_wide
        + times_transposed(hidden[0], point_weight)
        + times_transposed(hidden[1], other_point)
    ).astype(jnp.bfloat16)
    scores = times(block_out, whole_track)
    cotangent = track_cotangent.reshape(number_rows, whole_track.shape[1])
    score_grad = (cotangent.astype(jnp.float32) * jax.nn.sigmoid(scores)).astype(jnp.bfloat16)
    own_part = times_transposed(score_grad, whole_track).astype(jnp.bfloat16)
    out_grad = own_part.astype(jnp.float32) + head_swap(own_part).astype(jnp.float32)
    out_grad_b = out_grad.astype(jnp.bfloat16)
    hidden_grad = times(out_grad_b, point_weight)
    middle_gradient = (hidden_grad * gelu_slope(middle)).astype(jnp.bfloat16)
    later, earlier = halo_exchange(middle_gradient)
    taps = (later, middle_gradient, earlier)
    blocks = [transposed_times(out_grad_b, hidden[0])] + [
        transposed_times(activated, tap) for tap in taps
    ]
    blocks = [block.astype(jnp.bfloat16) for block in blocks]
    grads = jnp.stack(
        [jnp.concatenate(blocks[:2], axis=1), jnp.concatenate(blocks[2:], axis=1)], axis=0
    )
    act_part = sum(times_transposed(tap, weight) for tap, weight in zip(taps, taps_weight))
    act_part = act_part.astype(jnp.bfloat16)
    summed, act_other = reduce_and_swap(grads, act_part)
    act_grad = act_part.astype(jnp.float32) + act_other.astype(jnp.float32)
    input_grad = (out_grad + act_grad * gelu_slope(feat_wide)).astype(jnp.bfloat16)
    point_grad = summed[0, :, :width]
    dilated_grad = jnp.stack(
        [summed[0, :, width:], summed[1, :, :width], summed[1, :, width:]], axis=1
    )
    return (input_grad.reshape(samples, positions, channels), dilated_grad, point_grad)


def solution(mesh):
    torus = Mesh(
        mesh.devices.reshape(NZ, NY, 2, mesh.shape["head"], mesh.shape["sample"]),
        ("z", "y", "c", "h", "s"),
    )
    placed = (
        P("s", SEQ, None),
        P(None, None, "h"),
        P(None, "h"),
        P("s", "h"),
        P("s", SEQ, "h"),
    )
    return jax.shard_map(
        body,
        mesh=torus,
        in_specs=placed,
        out_specs=(P("s", SEQ, None), P(SEQ_SAMPLE, None, "h"), P(SEQ_SAMPLE, "h")),
        check_vma=False,
    )
```

time: 350 us -> 156 us (0.45)
  waiting for transfers between devices: 191 us -> 0 us
  Pallas kernels: 0 us -> 116 us
  blocking collectives: 60 us -> 0 us
  starting transfers between devices: 22.9 us -> 0 us
  local copies, waits for them, and re-layouts: 20.7 us -> 2.15 us
  between operations: 14 us -> 0.85 us
  other arithmetic: 18.3 us -> 6.63 us
  matrix products: 22.7 us -> 29.6 us
    unnamed x6 -> x0, waiting for transfers between devices: 119 us -> none
    pallas_call x0 -> x4, Pallas kernels: none -> 116 us  [the longest x1 46.5 us: reduce_and_swap(): pl.pallas_call(reduce_kernel, out_shape=(jax.ShapeDtypeStruct((2, each, w...]
    all_to_all x2 -> x0, blocking collectives: 60 us -> none  [from_everyone(): lax.all_to_all(jnp.broadcast_to(value[None], (size, *value.shape)), axis,...]
    ppermute x4 -> x0, waiting for transfers between devices: 35.5 us -> none  [passed_along(): lax.ppermute(value, axis, [(source, source + steps) for source in range(l...]
    all_gather x1 -> x0, waiting for transfers between devices: 21.1 us -> none  [body(): whole_track = lax.all_gather(track_weight, 'sample', axis=0, tiled=True)]
    unnamed x24 -> x23, local copies, waits for them, and re-layouts: 16.2 us -> 1.54 us
    ppermute x4 -> x0, starting transfers between devices: 13.9 us -> none  [passed_along(): lax.ppermute(value, axis, [(source, source + steps) for source in range(l...]
    dot_general x4 -> x5, matrix products: 3.82 us -> 15.2 us  [times(): return jnp.dot(left, right, preferred_element_type=jnp.float32)]
  transfers between devices with their start and end apart: 10 -> 0, of which waited for: 9 -> 0; matrix products, arithmetic and copies ran while one was open for 7% -> 0% of each run, Pallas kernels for 0% -> 0%
where the time goes in v1:
time: 156 us
  Pallas kernels  116 us (74%)
  matrix products  29.6 us (19%)
  other arithmetic  6.63 us (4%)
  local copies, waits for them, and re-layouts  2.15 us (1%)
    pallas_call x1, Pallas kernels, reduce_and_swap(): pl.pallas_call(reduce_kernel, out_shape=(jax.ShapeDtypeStruct((2, each, w...  46.5 us
    pallas_call x1, Pallas kernels, forward_exchange(): pl.pallas_call(forward_kernel, out_shape=(jax.ShapeDtypeStruct((rows, wid...  38 us
    pallas_call x1, Pallas kernels, head_swap(): pl.pallas_call(swap_kernel, out_shape=jax.ShapeDtypeStruct(mine.shape, mi...  21.2 us
    dot_general x5, matrix products, times(): return jnp.dot(left, right, preferred_element_type=jnp.float32)  15.2 us
    pallas_call x1, Pallas kernels, halo_exchange(): pl.pallas_call(halo_kernel, out_shape=(shape, shape), in_specs=[VMEM], ou...  10.9 us
    dot_general x5, matrix products, times_transposed(): lax.dot_general(left, right, (((1,), (1,)), ((), ())), preferred_element_...  9.92 us
    dot_general x4, matrix products, transposed_times(): lax.dot_general(left, right, (((0,), (0,)), ((), ())), preferred_element_...  4.49 us
    reshape x1, other arithmetic, body(): input_grad.reshape(samples, positions, channels)  3.44 us

profile of v1, /device:TPU:1, one launch (start us, length us, event | category | flops | bytes accessed | tf_op | source)
XLA Modules:
  0.0 155.7 jit_solution(13276526056006172902)
XLA Ops:
  0.6 0.0 copy-start.4
  0.7 3.1 %fusion.43.q0 = bf16[256,384]{1,0:T(8,128)(2,1)} fusion(bf16[1536,3,384]{2,0,1:T(8,128)(2,1)} %param.6, bf16[1,256,1536]{2,1,0:T(8,128)(2,1)} %param.5), kind=kOutput, calls=%fused_computation.63 | convolution fusion | flops 306020352 | bytes 2162688 | tf_op jit(solution)/shard_map/dot_general | solution.py:34
  3.7 1.4 fusion.46.q2
  5.1 1.5 fusion.34.centre
  6.6 38.0 %forward_exchange.1 = (f32[256,384]{1,0:T(8,128)}, bf16[2,256,384]{2,1,0:T(8,128)(2,1)}, bf16[2,768,1920]{2,1,0:T(8,128)(2,1)}, bf16[1536,384]{1,0:T(8,128)(2,1)}) custom-call(bf16[256,384]{1,0:T(8,128)(2,1)} %fusion.43.q0, bf16[256,384]{1,0:T(8,128)(2,1)} %fusion.46.q2, f32[256,384]{1,0:T(8,128)} %fusion.34.centre, bf16[768,1920]{1,0:T(8,128)(2,1)} %tw.1, ...), custom_call_target="tpu_custom_call" | custom-call | tf_op jit(solution)/shard_map/forward_exchange/pallas_call | solution.py:294
  44.6 1.5 fusion.7
  46.1 6.5 %fusion.14 = bf16[256,1920]{1,0:T(8,128)(2,1)} fusion(bf16[1536,1920]{1,0:T(8,128)(2,1)} %bitcast.124, f32[256,1536]{1,0:T(8,128)S(1)} %fusion.7, bf16[1536,384]{1,0:T(8,128)(2,1)} %get-tuple-element.12, bf16[1,256,1920]{2,1,0:T(8,128)(2,1)} %param.9, bf16[2,256,384]{2,1,0:T(8,128)(2,1)} %get-tuple-element.11), kind=kOutput, calls=%fused_computation.29 | convolution fusion | flops 1815674880 | bytes 10813440 | tf_op jit(solution)/shard_map/dot_general | solution.py:34
  52.6 5.7 %convolution_convert_fusion.4.mine = bf16[256,1536]{1,0:T(8,128)(2,1)} fusion(bf16[256,1920]{1,0:T(8,128)(2,1)} %fusion.14, bf16[1536,1920]{1,0:T(8,128)(2,1)} %bitcast.125), kind=kOutput, calls=%fused_computation.30 | convolution fusion | flops 1510342656 | bytes 7667712 | tf_op jit(solution)/shard_map/dot_general | solution.py:38
  58.3 21.2 %head_swap.1 = bf16[256,1536]{1,0:T(8,128)(2,1)} custom-call(bf16[256,1536]{1,0:T(8,128)(2,1)} %convolution_convert_fusion.4.mine), custom_call_target="tpu_custom_call" | custom-call | tf_op jit(solution)/shard_map/head_swap/pallas_call | solution.py:333
  79.5 2.7 %fusion.49.grad = bf16[256,384]{1,0:T(8,128)(2,1)} fusion(bf16[1536,384]{1,0:T(8,128)(2,1)S(1)} %copy-done.3, f32[256,384]{1,0:T(8,128)} %get-tuple-element.14, bf16[256,1536]{1,0:T(8,128)(2,1)} %head_swap.1, bf16[256,1536]{1,0:T(8,128)(2,1)S(1)} %copy-done), kind=kOutput, calls=%fused_computation.65 | convolution fusion | flops 305430528 | bytes 3342336 | tf_op jit(solution)/shard_map/dot_general | solution.py:34
  82.2 10.9 %halo_exchange.1 = (bf16[256,384]{1,0:T(8,128)(2,1)}, bf16[256,384]{1,0:T(8,128)(2,1)}) custom-call(bf16[256,384]{1,0:T(8,128)(2,1)} %fusion.49.grad), custom_call_target="tpu_custom_call" | custom-call | tf_op jit(solution)/shard_map/halo_exchange/pallas_call | solution.py:357
  93.1 1.6 %convolution_convert_fusion.3 = bf16[1536,384]{1,0:T(8,128)(2,1)S(1)} fusion(bf16[256,1536]{1,0:T(8,128)(2,1)S(1)} %copy-done.1, bf16[256,1536]{1,0:T(8,128)(2,1)S(1)} %copy-done, bf16[2,256,384]{2,1,0:T(8,128)(2,1)} %get-tuple-element.11), kind=kOutput, calls=%fused_computation.18 | convolution fusion | flops 304152576 | bytes 2949120 | tf_op jit(solution)/shard_map/dot_general | solution.py:44
  94.7 0.0 copy-done.9
  94.7 0.0 copy-start.8
  94.7 1.0 convolution_convert_fusion.2
  95.7 0.0 copy-start.7
  95.7 1.0 convolution_convert_fusion
  96.7 1.0 convolution_convert_fusion.1
  97.7 0.4 maximum_bitcast_fusion
  98.1 0.0 copy-start.5
  98.1 2.8 %pad_maximum_fusion.grads = bf16[2,1536,768]{2,1,0:T(8,128)(2,1)} fusion(bf16[1,1536,768]{2,1,0:T(8,128)(2,1)S(1)} %get-tuple-element.27, bf16[1,1536,768]{2,1,0:T(8,128)(2,1)S(1)} %get-tuple-element.26), kind=kLoop, calls=%fused_computation | loop fusion | flops 2359296 | bytes 9437184 | tf_op jit(solution)/shard_map/stack | solution.py:549
  100.9 0.8 copy-done.5
  101.7 0.6 fusion.39
  102.3 0.6 convolution_add_fusion.1
  102.9 1.5 fusion.13.act
  104.4 46.5 %reduce_and_swap.1 = (f32[2,12,768]{2,1,0:T(8,128)}, bf16[256,1536]{1,0:T(8,128)(2,1)}) custom-call(bf16[2,1536,768]{2,1,0:T(8,128)(2,1)} %pad_maximum_fusion.grads, bf16[256,1536]{1,0:T(8,128)(2,1)} %fusion.13.act), custom_call_target="tpu_custom_call" | custom-call | tf_op jit(solution)/shard_map/reduce_and_swap/pallas_call | solution.py:491
  150.9 0.0 copy-done.2
  150.9 0.0 copy-start.10
  150.9 3.4 %fusion.57 = bf16[1,256,1536]{2,1,0:T(8,128)(2,1)} fusion(bf16[1,256,1536]{2,1,0:T(8,128)(2,1)S(1)} %copy-done.6, bf16[256,1536]{1,0:T(8,128)(2,1)} %get-tuple-element.17, bf16[256,1536]{1,0:T(8,128)(2,1)S(1)} %copy-done.2, bf16[256,1536]{1,0:T(8,128)(2,1)S(1)} %copy-done.1, bf16[256,1536]{1,0:T(8,128)(2,1)S(1)} %copy-done), kind=kLoop, calls=%fused_computation.73 | loop fusion | flops 10616832 | bytes 4718592 | tf_op jit(solution)/shard_map/reshape | solution.py:561
  154.4 0.0 copy-done.10
  154.4 0.6 slice_bitcast_fusion
  155.0 0.7 copy.12
  (14 shorter events, 0.0 us)
Async XLA Ops:
  0.6 3.1 %copy-start.6 = (bf16[1,256,1536]{2,1,0:T(8,128)(2,1)S(1)}, bf16[1,256,1536]{2,1,0:T(8,128)(2,1)}, u32[]{:S(2)}) copy-start(bf16[1,256,1536]{2,1,0:T(8,128)(2,1)} %param.5) | copy-start | bytes 2359300
  0.6 3.1 %copy-start.4 = (bf16[1536,3,384]{2,0,1:T(8,128)(2,1)S(1)}, bf16[1536,3,384]{2,0,1:T(8,128)(2,1)}, u32[]{:S(2)}) copy-start(bf16[1536,3,384]{2,0,1:T(8,128)(2,1)} %param.6) | copy-start | bytes 10616836
  6.6 38.0 %copy-start.3 = (bf16[1536,384]{1,0:T(8,128)(2,1)S(1)}, bf16[1536,384]{1,0:T(8,128)(2,1)}, u32[]{:S(2)}) copy-start(bf16[1536,384]{1,0:T(8,128)(2,1)} %pw.1) | copy-start | bytes 3538948
  58.3 21.2 %copy-start = (bf16[256,1536]{1,0:T(8,128)(2,1)S(1)}, bf16[256,1536]{1,0:T(8,128)(2,1)}, u32[]{:S(2)}) copy-start(bf16[256,1536]{1,0:T(8,128)(2,1)} %convolution_convert_fusion.4.mine) | copy-start | bytes 2359300
  79.5 13.6 %copy-start.1 = (bf16[256,1536]{1,0:T(8,128)(2,1)S(1)}, bf16[256,1536]{1,0:T(8,128)(2,1)}, u32[]{:S(2)}) copy-start(bf16[256,1536]{1,0:T(8,128)(2,1)} %head_swap.1) | copy-start | bytes 2359300
  93.1 1.6 %copy-start.9 = (bf16[256,384]{1,0:T(8,128)(2,1)S(1)}, bf16[256,384]{1,0:T(8,128)(2,1)}, u32[]{:S(2)}) copy-start(bf16[256,384]{1,0:T(8,128)(2,1)} %get-tuple-element.15) | copy-start | bytes 589828
  94.7 1.0 copy-start.8
  95.7 1.0 copy-start.7
  98.1 3.6 %copy-start.5 = (bf16[1536,3,384]{2,0,1:T(8,128)(2,1)S(1)}, bf16[1536,3,384]{2,0,1:T(8,128)(2,1)}, u32[]{:S(2)}) copy-start(bf16[1536,3,384]{2,0,1:T(8,128)(2,1)} %param.6) | copy-start | bytes 10616836
  104.4 46.5 %copy-start.2 = (bf16[256,1536]{1,0:T(8,128)(2,1)S(1)}, bf16[256,1536]{1,0:T(8,128)(2,1)}, u32[]{:S(2)}) copy-start(bf16[256,1536]{1,0:T(8,128)(2,1)} %fusion.13.act) | copy-start | bytes 2359300
  150.9 3.5 %copy-start.10 = (f32[2,12,768]{2,1,0:T(8,128)S(1)}, f32[2,12,768]{2,1,0:T(8,128)}, u32[]{:S(2)}) copy-start(f32[2,12,768]{2,1,0:T(8,128)} %get-tuple-element.18) | copy-start | bytes 221188

commit v2 on v1

--- a/solution.py
+++ b/solution.py
@@ -11,7 +11,6 @@
 SEQ_SAMPLE = ("z", "y", "c", "s")
 NZ, NY = 8, 4
 YROWS, ZROWS = 64, 16
-SUBS = 4
 VMEM = pl.BlockSpec(memory_space=pltpu.VMEM)
 ANY = pl.BlockSpec(memory_space=pl.ANY)
 DMA = pltpu.SemaphoreType.DMA
@@ -319,207 +318,413 @@
     )(q0, q2, centre, tw, pw)
 
 
-def swap_kernel(mine, theirs, sent, arrived):
-    h = lax.axis_index("h")
-    barrier = pltpu.get_barrier_semaphore()
-    greet(barrier, h=1 - h)
-    pl.semaphore_wait(barrier, 1)
-    copy = remote(mine, theirs, sent, arrived, h=1 - h)
-    copy.start()
-    copy.wait()
-
-
-def head_swap(mine):
-    return pl.pallas_call(
-        swap_kernel,
-        out_shape=jax.ShapeDtypeStruct(mine.shape, mine.dtype),
-        in_specs=[VMEM],
-        out_specs=VMEM,
-        scratch_shapes=[DMA, DMA],
-        compiler_params=pltpu.CompilerParams(collective_id=1, has_side_effects=True),
-        name="head_swap",
-    )(mine)
-
-
-def halo_kernel(grad, later, earlier, sent, arrived):
-    z, y, c, h, s = place()
-    barrier = pltpu.get_barrier_semaphore()
-    count = greet_halo(barrier, z, y)
-    pl.semaphore_wait(barrier, count)
-    ahead, behind = (grad, earlier), (grad, later)
-    send_halo(z, y, ahead, behind, sent, arrived)
-    wait_halo(z, y, ahead, behind, sent, arrived)
-    drain_halo(z, y, ahead, behind, sent, arrived)
-
-
-def halo_exchange(grad):
-    shape = jax.ShapeDtypeStruct(grad.shape, grad.dtype)
-    return pl.pallas_call(
-        halo_kernel,
-        out_shape=(shape, shape),
-        in_specs=[VMEM],
-        out_specs=(VMEM, VMEM),
-        scratch_shapes=[DMA((2,)), DMA((2,))],
-        compiler_params=pltpu.CompilerParams(collective_id=2, has_side_effects=True),
-        name="halo_exchange",
-    )(grad)
-
-
-def reduce_kernel(
-    grads, act, summed, act_other,
-    sibling, sendbuf, recvbuf, final, last_send, last_recv,
-    act_s, act_r, sib_s, sib_r, ring_s, ring_r, last_s, last_r,
+COLS = 256
+HALVES, PIECES = 2, 2
+
+
+def cols_at(start, size):
+    return pl.ds(pl.multiple_of(start, 128), size)
+
+
+def repeat(count, step, start=0):
+    def once(at, carry):
+        step(at)
+        return carry
+
+    lax.fori_loop(start, count, once, 0)
+
+
+def backward_kernel(
+    feat, hidden, middle, act_t, tw, cot, pw, pwo, w3, grad_out, summed,
+    v_feat, v_act, v_tw, v_cot, v_pw, v_pwo, v_w3, block, score, out_grad, slope_f, slope_m,
+    hid_grad, mid_grad, later, earlier, swap_out, swap_in, act_out, act_in,
+    early, late, sib_early, sib_late, ring_out, ring_in, final, early_out, early_in,
+    y_out, y_in, z_tile, z_out, z_in,
+    load, tw_load, swap_s, swap_r, acts_s, acts_r, halo_s, halo_r, sibe_s, sibe_r, sibl_s, sibl_r,
+    ring_s, ring_r, fin_s, fin_r, y_s, y_r, z_s, z_r,
 ):
     z, y, c, h, s = place()
     up, down = lax.rem(z + 1, NZ), lax.rem(z + NZ - 1, NZ)
     me = (y * 2 + c) * 2 + s
+    corner = c * 2 + s
+    channels, tracks = tw.shape
+    chunks = channels // COLS
+    rows = channels // NZ
+    part = rows // NY
+    each = part // 4
+    sub = rows // HALVES // PIECES
+    bf16, f32 = jnp.bfloat16, jnp.float32
 
     def group(at):
         return {"y": lax.div(at, 4), "c": lax.rem(lax.div(at, 2), 2), "s": lax.rem(at, 2)}
 
+    def corner_of(at):
+        return {"c": lax.div(at, 2), "s": lax.rem(at, 2)}
+
     barrier = pltpu.get_barrier_semaphore()
-    greet(barrier, c=1 - c)
-    greet(barrier, z=up)
-    greet(barrier, z=down)
     greet(barrier, h=1 - h)
     for step in range(1, 16):
         greet(barrier, **group(lax.rem(me + step, 16)))
-    pl.semaphore_wait(barrier, 19)
-
-    rows = grads.shape[1] // NZ
-    width = grads.shape[2] // 2
-    sub = rows // SUBS
-    act_copy = remote(act, act_other, act_s, act_r, h=1 - h)
+    for step in range(1, NZ):
+        for turn in range(4):
+            greet(barrier, z=lax.rem(z + step, NZ), **corner_of(turn))
+    greeted = 1 + 15 + 4 * (NZ - 1) + greet_halo(barrier, z, y)
+
+    loads = [
+        pltpu.make_async_copy(source, target, load.at[slot])
+        for slot, (source, target) in enumerate(
+            ((feat, v_feat), (pw, v_pw), (pwo, v_pwo), (cot, v_cot), (act_t, v_act), (w3, v_w3))
+        )
+    ]
+    whole, tail = tracks // COLS, tracks % COLS
+
+    def tw_copy(at, size=COLS):
+        where = cols_at(at * COLS, size)
+        return pltpu.make_async_copy(tw.at[:, where], v_tw.at[:, where], tw_load.at[at])
+
+    for copy in loads[:3]:
+        copy.start()
+    repeat(whole, lambda at: tw_copy(at).start())
+    tw_copy(whole, tail).start()
+    for copy in loads[3:]:
+        copy.start()
+    for copy in loads[:3]:
+        copy.wait()
+
+    def block_step(at):
+        cols, where = cols_at(at * COLS, COLS), rows_at(at * COLS, COLS)
+        value = v_feat[:, cols].astype(f32)
+        value = value + times_transposed(hidden[0], v_pw[where, :])
+        value = value + times_transposed(hidden[1], v_pwo[where, :])
+        block[:, cols] = value.astype(bf16)
+
+    repeat(chunks, block_step)
+    loads[3].wait()
+
+    def score_step(at, size=COLS):
+        tw_copy(at, size).wait()
+        cols = cols_at(at * COLS, size)
+        value = jax.nn.sigmoid(times(block[...], v_tw[:, cols]))
+        score[:, cols] = (v_cot[:, cols].astype(f32) * value).astype(bf16)
+
+    repeat(whole, score_step)
+    score_step(whole, tail)
+    pl.semaphore_wait(barrier, greeted)
+
+    def swap_copy(at):
+        return remote(swap_out.at[at], swap_in.at[at], swap_s.at[at], swap_r.at[at], h=1 - h)
+
+    def swap_step(at):
+        swap_out[at] = times_transposed(score[...], v_tw[rows_at(at * COLS, COLS), :]).astype(bf16)
+        swap_copy(at).start()
+
+    repeat(chunks, swap_step)
+    slope_m[...] = gelu_slope(middle[...])
+    hid_grad[...] = jnp.zeros_like(hid_grad)
+
+    def slope_step(at):
+        cols = cols_at(at * COLS, COLS)
+        slope_f[at] = gelu_slope(v_feat[:, cols].astype(f32))
+
+    repeat(chunks, slope_step)
+
+    def gather_step(at):
+        swap_copy(at).wait_recv()
+        where = rows_at(at * COLS, COLS)
+        value = swap_out[at].astype(f32) + swap_in[at].astype(f32)
+        out_grad[at] = value
+        rounded = value.astype(bf16)
+        hid_grad[...] += times(rounded, v_pw[where, :])
+        early[0, where, :] = transposed_times(rounded, hidden[0]).astype(bf16)
+
+    repeat(chunks, gather_step)
+    mid_grad[...] = (hid_grad[...] * slope_m[...]).astype(bf16)
+    ahead, behind = (mid_grad, earlier), (mid_grad, later)
+    send_halo(z, y, ahead, behind, halo_s, halo_r)
+
+    loads[4].wait()
+
+    def centre_step(at):
+        where = rows_at(at * rows, rows)
+        early[1, where, :] = times(v_act[where, :], mid_grad[...]).astype(bf16)
+
+    repeat(NZ, centre_step)
     order = (7, 1, 6, 2, 5, 3, 4, 0)
-    siblings = []
-    for slot, offset in enumerate(order):
-        at = rows_at(lax.rem(z + offset, NZ) * rows, rows)
-        copy = remote(grads.at[1 - c, at], sibling.at[at], sib_s.at[slot], sib_r.at[slot], c=1 - c)
-        copy.start()
-        siblings.append(copy)
-    act_copy.start()
-
-    def columns(way):
-        return pl.ds(way * width, width)
+
+    def early_sibling(slot):
+        where = rows_at(lax.rem(z + order[slot], NZ) * rows, rows)
+        return remote(early.at[1 - c, where], sib_early.at[where], sibe_s.at[slot], sibe_r.at[slot], c=1 - c)
+
+    for slot in range(NZ):
+        early_sibling(slot).start()
 
     def partial(at, way, piece):
-        where = rows_at(at * rows + piece * sub, sub)
-        mine = grads[c, where, columns(way)].astype(jnp.float32)
-        return mine + sibling[where, columns(way)].astype(jnp.float32)
+        where = rows_at(at * rows + (way * PIECES + piece) * sub, sub)
+        return early[c, where, :].astype(f32) + sib_early[where, :].astype(f32)
 
     def ring_copy(step, way, piece):
         return remote(
-            sendbuf.at[step, way, piece], recvbuf.at[step, way, piece],
+            ring_out.at[step, way, piece], ring_in.at[step, way, piece],
             ring_s.at[step, way, piece], ring_r.at[step, way, piece], z=up if way == 0 else down,
         )
 
-    def target(step, way):
-        return lax.rem(z + 2 * NZ - 1 - step, NZ) if way == 0 else lax.rem(z + 1 + step, NZ)
-
     def ring_step(step):
-        for piece in range(SUBS):
-            for way in range(2):
-                value = partial(target(step, way), way, piece)
-                ring_copy(step - 1, way, piece).wait_recv()
-                value = value + recvbuf[step - 1, way, piece].astype(jnp.float32)
-                sendbuf[step, way, piece] = value.astype(jnp.bfloat16)
+        for piece in range(PIECES):
+            for way in range(HALVES):
+                at = lax.rem(z + NZ - 1 - step, NZ) if way == 0 else lax.rem(z + 1 + step, NZ)
+                value = partial(at, way, piece)
+                if step:
+                    ring_copy(step - 1, way, piece).wait_recv()
+                    value = value + ring_in[step - 1, way, piece].astype(f32)
+                ring_out[step, way, piece] = value.astype(bf16)
                 ring_copy(step, way, piece).start()
 
-    siblings[0].wait_recv()
-    siblings[1].wait_recv()
-    for piece in range(SUBS):
-        for way in range(2):
-            sendbuf[0, way, piece] = partial(target(0, way), way, piece).astype(jnp.bfloat16)
-            ring_copy(0, way, piece).start()
-    for copy in siblings[2:]:
-        copy.wait_recv()
-
-    def body(step, carry):
-        ring_step(step)
-        return carry
-
-    lax.fori_loop(1, NZ - 1, body, 0)
-    for piece in range(SUBS):
-        for way in range(2):
+    early_sibling(0).wait_recv()
+    early_sibling(1).wait_recv()
+    ring_step(0)
+    for slot in range(2, NZ):
+        early_sibling(slot).wait_recv()
+    ring_step(1)
+    ring_step(2)
+    wait_halo(z, y, ahead, behind, halo_s, halo_r)
+
+    def late_sibling(at):
+        where = rows_at(at * rows, rows)
+        return remote(late.at[1 - c, where], sib_late.at[where], sibl_s.at[at], sibl_r.at[at], c=1 - c)
+
+    def late_step(turn):
+        at = lax.rem(z + turn, NZ)
+        where = rows_at(at * rows, rows)
+        late[0, where, :] = times(v_act[where, :], later[...]).astype(bf16)
+        late[1, where, :] = times(v_act[where, :], earlier[...]).astype(bf16)
+        late_sibling(at).start()
+
+    def y_copy(at, step):
+        return remote(
+            y_out.at[at, rows_at(lax.rem(y + step, NY) * part, part)], y_in.at[at, step - 1],
+            y_s.at[at, step - 1], y_r.at[at, step - 1], y=lax.rem(y + step, NY),
+        )
+
+    def y_step(turn):
+        at = lax.rem(z + turn, NZ)
+        where = rows_at(at * rows, rows)
+        late_sibling(at).wait_recv()
+        y_out[at] = (late[c, where, :].astype(f32) + sib_late[where, :].astype(f32)).astype(bf16)
+        for step in range(1, NY):
+            y_copy(at, step).start()
+
+    def late_and_y_step(turn):
+        late_step(turn)
+        y_step(turn - 1)
+
+    late_step(1)
+    repeat(NZ + 1, late_and_y_step, 2)
+    y_step(NZ)
+    ring_step(3)
+    loads[5].wait()
+
+    def act_copy(at):
+        return remote(act_out.at[at], act_in.at[at], acts_s.at[at], acts_r.at[at], h=1 - h)
+
+    def act_step(at):
+        where = rows_at(at * COLS, COLS)
+        value = times_transposed(later[...], v_w3[0, where, :])
+        value = value + times_transposed(mid_grad[...], v_w3[1, where, :])
+        value = value + times_transposed(earlier[...], v_w3[2, where, :])
+        act_out[at] = value.astype(bf16)
+        act_copy(at).start()
+
+    repeat(chunks, act_step)
+    ring_step(4)
+
+    def z_copy(turn, at, twist):
+        to = lax.rem(corner + twist, 4)
+        return remote(
+            z_out.at[at, to], z_in.at[z, corner], z_s.at[turn - 1, twist], z_r.at[turn - 1, twist],
+            z=at, **corner_of(to),
+        )
+
+    def z_sum(turn):
+        at = lax.rem(z + turn, NZ)
+        where = rows_at(at * rows + y * part, part)
+        value = late[c, where, :].astype(f32) + sib_late[where, :].astype(f32)
+        for step in range(1, NY):
+            y_copy(at, step).wait_recv()
+            value = value + y_in[at, step - 1].astype(f32)
+        z_tile[...] = value
+        for to in range(4):
+            z_out[at, to] = z_tile[to * each:(to + 1) * each, :].astype(bf16)
+        return at
+
+    def z_step(turn):
+        at = z_sum(turn)
+        for twist in range(4):
+            z_copy(turn, at, twist).start()
+
+    z_step(1)
+    z_step(2)
+    ring_step(5)
+    z_step(3)
+    z_step(4)
+    ring_step(6)
+    z_step(5)
+    z_step(6)
+    z_step(7)
+    z_sum(NZ)
+    for twist in range(1, 4):
+        z_copy(NZ, z, twist).start()
+    z_in[z, corner] = z_out[z, corner]
+
+    for piece in range(PIECES):
+        for way in range(HALVES):
             value = partial(z, way, piece)
             ring_copy(NZ - 2, way, piece).wait_recv()
-            value = value + recvbuf[NZ - 2, way, piece].astype(jnp.float32)
-            final[pl.ds(piece * sub, sub), columns(way)] = value
-    each = rows // 16
+            value = value + ring_in[NZ - 2, way, piece].astype(f32)
+            final[(way * PIECES + piece) * sub:(way * PIECES + piece + 1) * sub, :] = value
     for at in range(16):
-        last_send[at] = final[at * each:(at + 1) * each, :].astype(jnp.bfloat16)
-    lasts = []
+        early_out[at] = final[at * each:(at + 1) * each, :].astype(bf16)
+
+    def fin_copy(step):
+        to = lax.rem(me + step, 16)
+        return remote(early_out.at[to], early_in.at[me], fin_s.at[step - 1], fin_r.at[step - 1], **group(to))
+
     for step in range(1, 16):
-        to = lax.rem(me + step, 16)
-        copy = remote(
-            last_send.at[to], last_recv.at[me], last_s.at[step - 1], last_r.at[step - 1], **group(to)
-        )
-        copy.start()
-        lasts.append(copy)
-    last_recv[me] = last_send[me]
+        fin_copy(step).start()
+    early_in[me] = early_out[me]
+
+    def out_step(at):
+        act_copy(at).wait_recv()
+        value = act_out[at].astype(f32) + act_in[at].astype(f32)
+        grad_out[:, cols_at(at * COLS, COLS)] = (out_grad[at] + value * slope_f[at]).astype(bf16)
+
+    repeat(chunks, out_step)
+    for turn in range(1, NZ + 1):
+        for twist in range(1 if turn == NZ else 0, 4):
+            source = lax.rem(z + 2 * NZ - turn, NZ)
+            ref = z_in.at[source, lax.rem(corner + 4 - twist, 4)]
+            remote(ref, ref, z_s.at[turn - 1, twist], z_r.at[turn - 1, twist], z=z).wait_recv()
+    for core in range(2):
+        total = jnp.zeros((each, hidden.shape[2]), f32)
+        for turn in range(NZ):
+            for sample in range(2):
+                total = total + z_in[turn, core * 2 + sample].astype(f32)
+        summed[2 + core] = total
     for step in range(1, 16):
-        source = lax.rem(me + 16 - step, 16)
-        remote(
-            last_send.at[source], last_recv.at[source], last_s.at[step - 1], last_r.at[step - 1], c=c
-        ).wait_recv()
+        ref = early_in.at[lax.rem(me + 16 - step, 16)]
+        remote(ref, ref, fin_s.at[step - 1], fin_r.at[step - 1], z=z).wait_recv()
     for core in range(2):
-        total = jnp.zeros((each, 2 * width), jnp.float32)
+        total = jnp.zeros((each, hidden.shape[2]), f32)
         for row in range(NY):
             for sample in range(2):
-                total = total + last_recv[(row * 2 + core) * 2 + sample].astype(jnp.float32)
+                total = total + early_in[(row * 2 + core) * 2 + sample].astype(f32)
         summed[core] = total
-    act_copy.wait()
-    for copy in siblings:
-        copy.wait_send()
-    for copy in lasts:
-        copy.wait_send()
-
-    def drain(step, carry):
-        for piece in range(SUBS):
-            for way in range(2):
+
+    def drain_chunks(at):
+        swap_copy(at).wait_send()
+        act_copy(at).wait_send()
+
+    repeat(chunks, drain_chunks)
+    drain_halo(z, y, ahead, behind, halo_s, halo_r)
+    for slot in range(NZ):
+        early_sibling(slot).wait_send()
+    for step in range(NZ - 1):
+        for piece in range(PIECES):
+            for way in range(HALVES):
                 ring_copy(step, way, piece).wait_send()
-        return carry
-
-    lax.fori_loop(0, NZ - 1, drain, 0)
-
-
-def reduce_and_swap(grads, act):
-    _, channels, width = grads.shape
+
+    def drain_late(at):
+        late_sibling(at).wait_send()
+        for step in range(1, NY):
+            y_copy(at, step).wait_send()
+
+    repeat(NZ, drain_late)
+    for turn in range(1, NZ + 1):
+        for twist in range(1 if turn == NZ else 0, 4):
+            z_copy(turn, lax.rem(z + turn, NZ), twist).wait_send()
+    for step in range(1, 16):
+        fin_copy(step).wait_send()
+
+
+def backward(feat, hidden, middle, act_t, tw, cot, pw, pwo, w3):
+    bf16, f32 = jnp.bfloat16, jnp.float32
+    positions, channels = feat.shape
+    width = pw.shape[1]
+    tracks = tw.shape[1]
+    chunks = channels // COLS
     rows = channels // NZ
-    each = rows // 16
-    sub = rows // SUBS
+    part = rows // NY
+    each = part // 4
+    sub = rows // HALVES // PIECES
+    ring = (NZ - 1, HALVES, PIECES)
+    tile = (chunks, positions, COLS)
     return pl.pallas_call(
-        reduce_kernel,
+        backward_kernel,
         out_shape=(
-            jax.ShapeDtypeStruct((2, each, width), jnp.float32),
-            jax.ShapeDtypeStruct(act.shape, act.dtype),
+            jax.ShapeDtypeStruct((positions, channels), bf16),
+            jax.ShapeDtypeStruct((4, each, width), f32),
         ),
-        in_specs=[VMEM, VMEM],
+        in_specs=[ANY, VMEM, VMEM, ANY, ANY, ANY, ANY, ANY, ANY],
         out_specs=(VMEM, VMEM),
         scratch_shapes=[
-            pltpu.VMEM((channels, width), jnp.bfloat16),
-            pltpu.VMEM((NZ - 1, 2, SUBS, sub, width // 2), jnp.bfloat16),
-            pltpu.VMEM((NZ - 1, 2, SUBS, sub, width // 2), jnp.bfloat16),
-            pltpu.VMEM((rows, width), jnp.float32),
-            pltpu.VMEM((16, each, width), jnp.bfloat16),
-            pltpu.VMEM((16, each, width), jnp.bfloat16),
-            DMA, DMA,
-            DMA((8,)), DMA((8,)),
-            DMA((NZ - 1, 2, SUBS)), DMA((NZ - 1, 2, SUBS)),
+            pltpu.VMEM(feat.shape, bf16),
+            pltpu.VMEM(act_t.shape, bf16),
+            pltpu.VMEM(tw.shape, bf16),
+            pltpu.VMEM(cot.shape, bf16),
+            pltpu.VMEM(pw.shape, bf16),
+            pltpu.VMEM(pwo.shape, bf16),
+            pltpu.VMEM(w3.shape, bf16),
+            pltpu.VMEM((positions, channels), bf16),
+            pltpu.VMEM((positions, tracks), bf16),
+            pltpu.VMEM(tile, f32),
+            pltpu.VMEM(tile, f32),
+            pltpu.VMEM((positions, width), f32),
+            pltpu.VMEM((positions, width), f32),
+            pltpu.VMEM((positions, width), bf16),
+            pltpu.VMEM((positions, width), bf16),
+            pltpu.VMEM((positions, width), bf16),
+            pltpu.VMEM(tile, bf16),
+            pltpu.VMEM(tile, bf16),
+            pltpu.VMEM(tile, bf16),
+            pltpu.VMEM(tile, bf16),
+            pltpu.VMEM((2, channels, width), bf16),
+            pltpu.VMEM((2, channels, width), bf16),
+            pltpu.VMEM((channels, width), bf16),
+            pltpu.VMEM((channels, width), bf16),
+            pltpu.VMEM((*ring, sub, width), bf16),
+            pltpu.VMEM((*ring, sub, width), bf16),
+            pltpu.VMEM((rows, width), f32),
+            pltpu.VMEM((16, each, width), bf16),
+            pltpu.VMEM((16, each, width), bf16),
+            pltpu.VMEM((NZ, rows, width), bf16),
+            pltpu.VMEM((NZ, NY - 1, part, width), bf16),
+            pltpu.VMEM((part, width), f32),
+            pltpu.VMEM((NZ, 4, each, width), bf16),
+            pltpu.VMEM((NZ, 4, each, width), bf16),
+            DMA((6,)), DMA((tracks // COLS + 1,)),
+            DMA((chunks,)), DMA((chunks,)),
+            DMA((chunks,)), DMA((chunks,)),
+            DMA((2,)), DMA((2,)),
+            DMA((NZ,)), DMA((NZ,)),
+            DMA((NZ,)), DMA((NZ,)),
+            DMA(ring), DMA(ring),
             DMA((15,)), DMA((15,)),
+            DMA((NZ, NY - 1)), DMA((NZ, NY - 1)),
+            DMA((NZ, 4)), DMA((NZ, 4)),
         ],
-        compiler_params=pltpu.CompilerParams(collective_id=3, has_side_effects=True),
-        name="reduce_and_swap",
-    )(grads, act)
+        compiler_params=pltpu.CompilerParams(
+            collective_id=1, has_side_effects=True, vmem_limit_bytes=60 * 1024 * 1024
+        ),
+        name="backward",
+    )(feat, hidden, middle, act_t, tw, cot, pw, pwo, w3)
 
 
 def body(features, dilated_weight, point_weight, track_weight, track_cotangent):
     samples, positions, channels = features.shape
     number_rows = samples * positions
     width = dilated_weight.shape[2]
-    feat_wide = features.reshape(number_rows, channels).astype(jnp.float32)
-    activated = gelu_value(feat_wide).astype(jnp.bfloat16)
-    taps_weight = [dilated_weight[:, tap, :] for tap in range(3)]
+    feat = features.reshape(number_rows, channels)
+    activated = gelu_value(feat.astype(jnp.float32)).astype(jnp.bfloat16)
+    taps_weight = jnp.transpose(dilated_weight, (1, 0, 2))
     to_later = times(activated, taps_weight[0]).astype(jnp.bfloat16)
     to_earlier = times(activated, taps_weight[2]).astype(jnp.bfloat16)
     centre = times(activated, taps_weight[1])
@@ -527,38 +732,13 @@
         to_later, to_earlier, centre, track_weight, point_weight
     )
     whole_track = whole_track.reshape(channels, track_weight.shape[1])
-    block_out = (
-        feat_wide
-        + times_transposed(hidden[0], point_weight)
-        + times_transposed(hidden[1], other_point)
-    ).astype(jnp.bfloat16)
-    scores = times(block_out, whole_track)
     cotangent = track_cotangent.reshape(number_rows, whole_track.shape[1])
-    score_grad = (cotangent.astype(jnp.float32) * jax.nn.sigmoid(scores)).astype(jnp.bfloat16)
-    own_part = times_transposed(score_grad, whole_track).astype(jnp.bfloat16)
-    out_grad = own_part.astype(jnp.float32) + head_swap(own_part).astype(jnp.float32)
-    out_grad_b = out_grad.astype(jnp.bfloat16)
-    hidden_grad = times(out_grad_b, point_weight)
-    middle_gradient = (hidden_grad * gelu_slope(middle)).astype(jnp.bfloat16)
-    later, earlier = halo_exchange(middle_gradient)
-    taps = (later, middle_gradient, earlier)
-    blocks = [transposed_times(out_grad_b, hidden[0])] + [
-        transposed_times(activated, tap) for tap in taps
-    ]
-    blocks = [block.astype(jnp.bfloat16) for block in blocks]
-    grads = jnp.stack(
-        [jnp.concatenate(blocks[:2], axis=1), jnp.concatenate(blocks[2:], axis=1)], axis=0
-    )
-    act_part = sum(times_transposed(tap, weight) for tap, weight in zip(taps, taps_weight))
-    act_part = act_part.astype(jnp.bfloat16)
-    summed, act_other = reduce_and_swap(grads, act_part)
-    act_grad = act_part.astype(jnp.float32) + act_other.astype(jnp.float32)
-    input_grad = (out_grad + act_grad * gelu_slope(feat_wide)).astype(jnp.bfloat16)
-    point_grad = summed[0, :, :width]
-    dilated_grad = jnp.stack(
-        [summed[0, :, width:], summed[1, :, :width], summed[1, :, width:]], axis=1
-    )
-    return (input_grad.reshape(samples, positions, channels), dilated_grad, point_grad)
+    input_grad, summed = backward(
+        feat, hidden, middle, activated.T, whole_track, cotangent, point_weight, other_point,
+        taps_weight,
+    )
+    dilated_grad = jnp.stack([summed[2], summed[1], summed[3]], axis=1)
+    return (input_grad.reshape(samples, positions, channels), dilated_grad, summed[0])
 
 
 def solution(mesh):

time: 156 us -> 127 us (0.81)
  matrix products: 29.6 us -> 5.93 us
  other arithmetic: 6.63 us -> 1.42 us
  local copies, waits for them, and re-layouts: 2.15 us -> 4.42 us
  Pallas kernels: 116 us -> 114 us
    dot_general x9 -> x0, matrix products: 14.4 us -> none  [the longest x5 9.92 us: times_transposed(): lax.dot_general(left, right, (((1,), (1,)), ((), ())), preferred_element_...]
    dot_general x5 -> x3, matrix products: 15.2 us -> 5.93 us  [times(): return jnp.dot(left, right, preferred_element_type=jnp.float32)]
    reshape x1 -> x0, other arithmetic: 3.44 us -> none  [body(): input_grad.reshape(samples, positions, channels)]
    another operation x3 -> x1, other arithmetic: 3.19 us -> 0.01 us  [body(): dilated_grad = jnp.stack([summed[2], summed[1], summed[3]], axis=1)]
    pallas_call x3 -> x1, Pallas kernels: 78.5 us -> 75.9 us  [backward(): pl.pallas_call(backward_kernel, out_shape=(jax.ShapeDtypeStruct((position...]
where the time goes in v2:
time: 127 us; the launch traced here: 126 us
  Pallas kernels  114 us (90%)
  matrix products  5.93 us (5%)
  local copies, waits for them, and re-layouts  4.42 us (3%)
  other arithmetic  1.42 us (1%)
    pallas_call x1, Pallas kernels, backward(): pl.pallas_call(backward_kernel, out_shape=(jax.ShapeDtypeStruct((position...  75.9 us
    pallas_call x1, Pallas kernels, forward_exchange(): pl.pallas_call(forward_kernel, out_shape=(jax.ShapeDtypeStruct((rows, wid...  37.9 us
    dot_general x3, matrix products, times(): return jnp.dot(left, right, preferred_element_type=jnp.float32)  5.93 us
    unnamed x7, local copies, waits for them, and re-layouts  3.01 us

profile of v2, /device:TPU:1, one launch (start us, length us, event | category | flops | bytes accessed | tf_op | source)
XLA Modules:
  0.0 126.3 jit_solution(17503444301878830039)
XLA Ops:
  0.6 0.0 copy-start
  0.6 0.0 copy-start.1
  0.7 3.1 %fusion.14.q2 = bf16[256,384]{1,0:T(8,128)(2,1)} fusion(bf16[3,1536,384]{2,1,0:T(8,128)(2,1)} %bitcast.36, bf16[1,256,1536]{2,1,0:T(8,128)(2,1)} %param.5), kind=kOutput, calls=%fused_computation.27 | convolution fusion | flops 306020352 | bytes 2162688 | tf_op jit(solution)/shard_map/dot_general | solution.py:33
  3.7 0.0 copy-done
  3.7 0.0 copy-done.1
  3.7 1.4 %fusion.13.q0 = bf16[256,384]{1,0:T(8,128)(2,1)} fusion(bf16[3,1536,384]{2,1,0:T(8,128)(2,1)S(1)} %bitcast.38, bf16[1,256,1536]{2,1,0:T(8,128)(2,1)S(1)} %copy-done.1), kind=kOutput, calls=%fused_computation.26 | convolution fusion | flops 306020352 | bytes 2162688 | tf_op jit(solution)/shard_map/dot_general | solution.py:33
  5.1 1.5 %fusion.10.centre = f32[256,384]{1,0:T(8,128)} fusion(bf16[3,1536,384]{2,1,0:T(8,128)(2,1)S(1)} %bitcast.39, bf16[1,256,1536]{2,1,0:T(8,128)(2,1)S(1)} %copy-done.1), kind=kOutput, calls=%fused_computation.21 | convolution fusion | flops 305922048 | bytes 2359296 | tf_op jit(solution)/shard_map/dot_general | solution.py:33
  6.6 0.3 copy.8
  6.9 1.4 %fusion.15.act_t = bf16[1536,256]{1,0:T(8,128)(2,1)} fusion(bf16[1,256,1536]{1,2,0:T(8,128)(2,1)S(1)} %copy.8), kind=kLoop, calls=%fused_computation.28 | loop fusion | flops 3932160 | bytes 1572864 | tf_op jit(solution)/shard_map/transpose | solution.py:737
  8.3 37.9 %forward_exchange.1 = (f32[256,384]{1,0:T(8,128)}, bf16[2,256,384]{2,1,0:T(8,128)(2,1)}, bf16[2,768,1920]{2,1,0:T(8,128)(2,1)}, bf16[1536,384]{1,0:T(8,128)(2,1)}) custom-call(bf16[256,384]{1,0:T(8,128)(2,1)} %fusion.13.q0, bf16[256,384]{1,0:T(8,128)(2,1)} %fusion.14.q2, f32[256,384]{1,0:T(8,128)} %fusion.10.centre, bf16[768,1920]{1,0:T(8,128)(2,1)} %tw.1, ...), custom_call_target="tpu_custom_call" | custom-call | tf_op jit(solution)/shard_map/forward_exchange/pallas_call | solution.py:293
  46.2 75.9 %backward.1 = (bf16[256,1536]{1,0:T(8,128)(2,1)}, f32[4,12,384]{2,1,0:T(8,128)}) custom-call(bf16[256,1536]{1,0:T(8,128)(2,1)} %bitcast.40, bf16[2,256,384]{2,1,0:T(8,128)(2,1)} %get-tuple-element.9.hidden, f32[256,384]{1,0:T(8,128)} %get-tuple-element.10.middle, bf16[1536,256]{1,0:T(8,128)(2,1)} %fusion.15.act_t, bf16[1536,1920]{1,0:T(8,128)(2,1)} %bitcast.35, ...), custom_call_target="tpu_custom_call" | custom-call | tf_op jit(solution)/shard_map/backward/pallas_call | solution.py:660
  122.1 1.4 %slice_bitcast_fusion.10 = (f32[12,384]{1,0:T(8,128)}, f32[12,1,384]{2,0,1:T(8,128)S(1)}, f32[12,1,384]{2,0,1:T(8,128)S(1)}, f32[12,1,384]{2,0,1:T(8,128)S(1)}) fusion(f32[4,12,384]{2,1,0:T(8,128)} %get-tuple-element.14), kind=kLoop, calls=%fused_computation.31 | loop fusion | bytes 147456 | tf_op jit(solution)/shard_map/squeeze | solution.py:741
  123.6 0.7 copy.10
  124.2 2.1 %copy.13 = bf16[1,256,1536]{2,1,0:T(8,128)(2,1)} copy(bf16[1,256,1536]{2,1,0:T(8,128)(2,1)} %bitcast.42) | data formatting | bytes 1572864
  (1 shorter events, 0.0 us)
Async XLA Ops:
  0.6 3.1 %copy-start = (bf16[1536,3,384]{2,0,1:T(8,128)(2,1)S(1)}, bf16[1536,3,384]{2,0,1:T(8,128)(2,1)}, u32[]{:S(2)}) copy-start(bf16[1536,3,384]{2,0,1:T(8,128)(2,1)} %param.6) | copy-start | bytes 10616836
  0.6 3.1 %copy-start.1 = (bf16[1,256,1536]{2,1,0:T(8,128)(2,1)S(1)}, bf16[1,256,1536]{2,1,0:T(8,128)(2,1)}, u32[]{:S(2)}) copy-start(bf16[1,256,1536]{2,1,0:T(8,128)(2,1)} %param.5) | copy-start | bytes 2359300

commit v3 on v2

--- a/solution.py
+++ b/solution.py
@@ -10,9 +10,8 @@
 SEQ = ("z", "y", "c")
 SEQ_SAMPLE = ("z", "y", "c", "s")
 NZ, NY = 8, 4
-YROWS, ZROWS = 64, 16
 VMEM = pl.BlockSpec(memory_space=pltpu.VMEM)
-ANY = pl.BlockSpec(memory_space=pl.ANY)
+ANY = pl.BlockSpec(memory_space=pltpu.HBM)
 DMA = pltpu.SemaphoreType.DMA
 
 
@@ -136,207 +135,257 @@
     return before.astype(jnp.int32) + after.astype(jnp.int32)
 
 
+COLS = 256
+HALVES, PIECES = 2, 2
+
+
+def cols_at(start, size):
+    return pl.ds(pl.multiple_of(start, 128), size)
+
+
+def repeat(count, step, start=0):
+    def once(at, carry):
+        step(at)
+        return carry
+
+    lax.fori_loop(start, count, once, 0)
+
+
+YROWS, ZROWS, ZCUT = 40, 56, 32
+
+
 def forward_kernel(
-    q0, q2, centre, tw, pw, middle, hidden, twf, pwo,
-    from_before, from_after, own, own_sem,
-    halo_s, halo_r, hid_s, hid_r, x_s, x_r, y_s, y_r, tz_s, tz_r, pz_s, pz_r, sib_s, sib_r,
+    feat, w3, tw, pw, middle, hid_own, block, act_t, twf,
+    v_feat, v_w3, v_pw, own, act, ahead_out, behind_out, from_before, from_after, centre, hid_other, pwo,
+    load, own_sem, halo_s, halo_r, hid_s, hid_r, x_s, x_r, y_s, y_r, pz_s, pz_r, tz_s, tz_r, sib_s, sib_r,
 ):
     z, y, c, h, s = place()
-    up, down = lax.rem(z + 1, NZ), lax.rem(z + NZ - 1, NZ)
+    bf16, f32 = jnp.bfloat16, jnp.float32
+    channels = feat.shape[1]
+    chunks = channels // COLS
     barrier = pltpu.get_barrier_semaphore()
     greet(barrier, h=1 - h)
     greet(barrier, s=1 - s)
     greet(barrier, c=1 - c)
-    greet(barrier, z=up)
-    greet(barrier, z=down)
+    for step in (1, 2, NZ - 2, NZ - 1):
+        greet(barrier, z=lax.rem(z + step, NZ))
     for step in range(1, NY):
         greet(barrier, y=lax.rem(y + step, NY))
-    count = greet_halo(barrier, z, y)
-    pl.semaphore_wait(barrier, 8 + count)
-
-    half = tw.shape[0] // 2
-    pw_rows = pw.shape[0] // 2 // NZ
-    base = c * half
-
-    def y_piece(at):
-        return rows_at(base + at * YROWS, YROWS)
-
-    def z_piece(at):
-        return rows_at(base + NY * YROWS + at * ZROWS, ZROWS)
-
-    def p_piece(at):
-        return rows_at(c * (pw.shape[0] // 2) + at * pw_rows, pw_rows)
-
-    ahead, behind = (q0, from_before), (q2, from_after)
-    send_halo(z, y, ahead, behind, halo_s, halo_r)
-    to_sample = [
-        remote(tw.at[z_piece(z)], twf.at[s, z_piece(z)], x_s.at[0], x_r.at[0], s=1 - s),
-        remote(tw.at[y_piece(y)], twf.at[s, y_piece(y)], x_s.at[1], x_r.at[1], s=1 - s),
+    greeted = 10 + greet_halo(barrier, z, y)
+    loads = [
+        pltpu.make_async_copy(source, target, load.at[slot])
+        for slot, (source, target) in enumerate(
+            ((feat, v_feat), (w3.at[0], v_w3.at[0]), (w3.at[2], v_w3.at[2]), (w3.at[1], v_w3.at[1]), (pw, v_pw))
+        )
     ]
-    to_head = remote(pw.at[p_piece(z)], pwo.at[p_piece(z)], x_s.at[2], x_r.at[2], h=1 - h)
-    to_sample[0].start()
-    to_head.start()
-    to_sample[1].start()
+    for copy in loads:
+        copy.start()
     take_own = pltpu.make_async_copy(tw, own, own_sem.at[0])
     take_own.start()
 
-    started = [*to_sample, to_head]
-    landed = []
+    half = tw.shape[0] // 2
+    point = pw.shape[0] // 2
+    p_rows = point // 4
     other = 1 - s
 
-    def track_sibling(rows, slot):
-        copy = remote(twf.at[other, rows], twf.at[other, rows], sib_s.at[slot], sib_r.at[slot], c=1 - c)
+    def rows8(start, size):
+        return pl.ds(pl.multiple_of(start, 8), size)
+
+    def y_rows(core, at):
+        return rows8(core * half + at * YROWS, YROWS)
+
+    def z_rows(core, at, cut):
+        start = core * half + NY * YROWS + lax.rem(at, 4) * ZROWS
+        return rows8(start, ZCUT) if cut == 0 else rows8(start + ZCUT, ZROWS - ZCUT)
+
+    def p_rows_of(core, at, cut):
+        start = core * point + lax.rem(at, 4) * p_rows
+        if cut is None:
+            return rows8(start, p_rows)
+        return rows8(start + cut * (p_rows // 2), p_rows // 2)
+
+    started = []
+
+    def go(ref, target, sent, arrived, **device):
+        copy = remote(ref, target, sent, arrived, **device)
         copy.start()
         started.append(copy)
 
-    def point_sibling(rows, slot):
-        copy = remote(pwo.at[rows], pwo.at[rows], sib_s.at[slot], sib_r.at[slot], c=1 - c)
-        copy.start()
-        started.append(copy)
-
-    def send_z(at, slot, target):
-        rows = z_piece(at)
-        copy = remote(twf.at[other, rows], twf.at[other, rows], tz_s.at[slot], tz_r.at[slot], z=target)
-        copy.start()
-        started.append(copy)
-
-    def send_p(at, slot, target):
-        rows = p_piece(at)
-        copy = remote(pwo.at[rows], pwo.at[rows], pz_s.at[slot], pz_r.at[slot], z=target)
-        copy.start()
-        started.append(copy)
-
-    to_sample[0].wait_recv()
-    send_z(z, 0, up)
-    send_z(z, 4, down)
-    to_head.wait_recv()
-    send_p(z, 0, up)
-    send_p(z, 4, down)
-    track_sibling(z_piece(z), 0)
-    point_sibling(p_piece(z), 8)
-
+    def landing(ref, sent, arrived):
+        remote(ref, ref, sent, arrived, c=1 - c).wait_recv()
+
+    pl.semaphore_wait(barrier, greeted)
+    here = p_rows_of(c, z, None)
+    go(pw.at[here], pwo.at[here], x_s.at[0], x_r.at[0], h=1 - h)
+    for cut in range(2):
+        here = z_rows(c, z, cut)
+        go(tw.at[here], twf.at[s, here], x_s.at[1 + cut], x_r.at[1 + cut], s=1 - s)
+    here = y_rows(c, y)
+    go(tw.at[here], twf.at[s, here], x_s.at[3], x_r.at[3], s=1 - s)
+
+    loads[0].wait()
+
+    def act_step(at):
+        cols = cols_at(at * COLS, COLS)
+        act[:, cols] = gelu_value(v_feat[:, cols].astype(f32)).astype(bf16)
+
+    repeat(chunks, act_step)
+    before, after = has_neighbours(z, y)
+    ahead, behind = (ahead_out, from_before), (behind_out, from_after)
+    loads[1].wait()
+    ahead_out[...] = times(act[...], v_w3[0]).astype(bf16)
+
+    @pl.when(after)
+    def _():
+        remote(*ahead, halo_s.at[0], halo_r.at[0], **shifted(z, y, 2)).start()
+
+    loads[2].wait()
+    behind_out[...] = times(act[...], v_w3[2]).astype(bf16)
+
+    @pl.when(before)
+    def _():
+        remote(*behind, halo_s.at[1], halo_r.at[1], **shifted(z, y, -2)).start()
+
+    steps = (1, NZ - 1, 2, NZ - 2)
+    here = pwo.at[p_rows_of(c, z, None)]
+    landing(here, x_s.at[0], x_r.at[0])
+    for slot in range(2):
+        go(here, here, pz_s.at[slot], pz_r.at[slot], z=lax.rem(z + steps[slot], NZ))
+    for cut in range(2):
+        piece = pwo.at[p_rows_of(c, z, cut)]
+        go(piece, piece, pz_s.at[2 + cut], pz_r.at[2 + cut], z=lax.rem(z + steps[2 + cut], NZ))
+    go(here, here, sib_s.at[0], sib_r.at[0], c=1 - c)
+    for cut in range(2):
+        here = twf.at[other, z_rows(c, z, cut)]
+        landing(here, x_s.at[1 + cut], x_r.at[1 + cut])
+        for slot, step in enumerate((steps[0], steps[1], steps[2 + cut])):
+            go(here, here, tz_s.at[cut, slot], tz_r.at[cut, slot], z=lax.rem(z + step, NZ))
+        go(here, here, sib_s.at[5 + cut], sib_r.at[5 + cut], c=1 - c)
+        if cut == 0:
+            loads[3].wait()
+            centre[...] = times(act[...], v_w3[1])
+    here = twf.at[other, y_rows(c, y)]
+    landing(here, x_s.at[3], x_r.at[3])
+    for step in range(1, NY):
+        go(here, here, y_s.at[step - 1], y_r.at[step - 1], y=lax.rem(y + step, NY))
+    go(here, here, sib_s.at[13], sib_r.at[13], c=1 - c)
     take_own.wait()
     put_own = pltpu.make_async_copy(own, twf.at[s], own_sem.at[1])
     put_own.start()
 
-    def ring_step(step):
-        for send, sem_s, sem_r, buf, piece, slot, sibling, first in (
-            (send_z, tz_s, tz_r, None, z_piece, 0, track_sibling, 0),
-            (send_p, pz_s, pz_r, pwo, p_piece, 0, point_sibling, 8),
-        ):
-            ref = twf.at[other] if buf is None else buf
-            at = lax.rem(z + NZ - step, NZ)
-            remote(ref.at[piece(at)], ref.at[piece(at)], sem_s.at[step - 1], sem_r.at[step - 1], z=up).wait_recv()
-            if step < 4:
-                send(at, step, up)
-            sibling(piece(at), first + step)
-            if step < 4:
-                at = lax.rem(z + step, NZ)
-                remote(ref.at[piece(at)], ref.at[piece(at)], sem_s.at[step + 3], sem_r.at[step + 3], z=up).wait_recv()
-                if step < 3:
-                    send(at, 4 + step, down)
-                sibling(piece(at), first + 4 + step)
-
-    ring_step(1)
-    to_sample[1].wait_recv()
-    rows = y_piece(y)
+    def turn_step(at):
+        act_t[rows_at(at * COLS, COLS), :] = act[:, cols_at(at * COLS, COLS)].T
+
+    repeat(chunks, turn_step)
+
+    def p_from(core, slot):
+        at = z + NZ - steps[slot]
+        return pwo.at[p_rows_of(core, at, None if slot < 2 else slot - 2)]
+
+    def t_from(core, cut, slot):
+        step = steps[slot] if slot < 2 else steps[2 + cut]
+        return twf.at[other, z_rows(core, z + NZ - step, cut)]
+
+    def y_from(core, step):
+        return twf.at[other, y_rows(core, lax.rem(y + NY - step, NY))]
+
+    for slot in range(4):
+        here = p_from(c, slot)
+        landing(here, pz_s.at[slot], pz_r.at[slot])
+        go(here, here, sib_s.at[1 + slot], sib_r.at[1 + slot], c=1 - c)
+
+    wait_halo(z, y, ahead, behind, halo_s, halo_r)
+    total = centre[...] + from_before[...].astype(f32) + from_after[...].astype(f32)
+    middle[...] = total
+    hid_own[...] = gelu_value(total).astype(bf16)
+    go(hid_own, hid_other, hid_s, hid_r, h=1 - h)
+
+    for cut in range(2):
+        for slot in range(3):
+            here = t_from(c, cut, slot)
+            landing(here, tz_s.at[cut, slot], tz_r.at[cut, slot])
+            at = 7 + cut * 3 + slot
+            go(here, here, sib_s.at[at], sib_r.at[at], c=1 - c)
     for step in range(1, NY):
-        copy = remote(
-            twf.at[other, rows], twf.at[other, rows], y_s.at[step - 1], y_r.at[step - 1],
-            y=lax.rem(y + step, NY),
-        )
-        copy.start()
-        started.append(copy)
-    track_sibling(rows, 16)
-    ring_step(2)
-
-    wait_halo(z, y, ahead, behind, halo_s, halo_r)
-    total = centre[...] + from_before[...].astype(jnp.float32) + from_after[...].astype(jnp.float32)
-    middle[...] = total
-    hidden[0] = gelu_value(total).astype(jnp.bfloat16)
-    to_partner = remote(hidden.at[0], hidden.at[1], hid_s, hid_r, h=1 - h)
-    to_partner.start()
-    started.append(to_partner)
-    ring_step(3)
-    ring_step(4)
+        here = y_from(c, step)
+        landing(here, y_s.at[step - 1], y_r.at[step - 1])
+        go(here, here, sib_s.at[13 + step], sib_r.at[13 + step], c=1 - c)
+
+    landing(pwo.at[p_rows_of(1 - c, z, None)], sib_s.at[0], sib_r.at[0])
+    for slot in range(4):
+        landing(p_from(1 - c, slot), sib_s.at[1 + slot], sib_r.at[1 + slot])
+    loads[4].wait()
+    landing(hid_other, hid_s, hid_r)
+
+    def block_step(at):
+        cols, where = cols_at(at * COLS, COLS), rows_at(at * COLS, COLS)
+        value = v_feat[:, cols].astype(f32)
+        value = value + times_transposed(hid_own[...], v_pw[where, :])
+        value = value + times_transposed(hid_other[...], pwo[where, :])
+        block[:, cols] = value.astype(bf16)
+
+    repeat(chunks, block_step)
+    for cut in range(2):
+        landing(twf.at[other, z_rows(1 - c, z, cut)], sib_s.at[5 + cut], sib_r.at[5 + cut])
+        for slot in range(3):
+            at = 7 + cut * 3 + slot
+            landing(t_from(1 - c, cut, slot), sib_s.at[at], sib_r.at[at])
+    landing(twf.at[other, y_rows(1 - c, y)], sib_s.at[13], sib_r.at[13])
     for step in range(1, NY):
-        rows = y_piece(lax.rem(y + NY - step, NY))
-        remote(
-            twf.at[other, rows], twf.at[other, rows], y_s.at[step - 1], y_r.at[step - 1], y=y
-        ).wait_recv()
-        track_sibling(rows, 16 + step)
-    to_partner.wait_recv()
-
-    sib_base = (1 - c) * half
-    sib_point = (1 - c) * (pw.shape[0] // 2)
-    for slot in range(20):
-        step = slot % 8 if slot < 16 else slot - 16
-        if slot < 16:
-            at = lax.rem(z + NZ - step, NZ) if step <= 4 else lax.rem(z + step - 4, NZ)
-        else:
-            at = lax.rem(y + NY - step, NY)
-        if slot < 8:
-            ref = twf.at[other, rows_at(sib_base + NY * YROWS + at * ZROWS, ZROWS)]
-        elif slot < 16:
-            ref = pwo.at[rows_at(sib_point + at * pw_rows, pw_rows)]
-        else:
-            ref = twf.at[other, rows_at(sib_base + at * YROWS, YROWS)]
-        remote(ref, ref, sib_s.at[slot], sib_r.at[slot], c=1 - c).wait_recv()
+        landing(y_from(1 - c, step), sib_s.at[13 + step], sib_r.at[13 + step])
     for copy in started:
         copy.wait_send()
     drain_halo(z, y, ahead, behind, halo_s, halo_r)
     put_own.wait()
 
 
-def forward_exchange(q0, q2, centre, tw, pw):
-    rows, width = q0.shape
+def forward_exchange(feat, w3, tw, pw):
+    bf16, f32 = jnp.bfloat16, jnp.float32
+    positions, channels = feat.shape
+    width = pw.shape[1]
     return pl.pallas_call(
         forward_kernel,
         out_shape=(
-            jax.ShapeDtypeStruct((rows, width), jnp.float32),
-            jax.ShapeDtypeStruct((2, rows, width), jnp.bfloat16),
-            jax.ShapeDtypeStruct((2, *tw.shape), jnp.bfloat16),
-            jax.ShapeDtypeStruct(pw.shape, jnp.bfloat16),
+            jax.ShapeDtypeStruct((positions, width), f32),
+            jax.ShapeDtypeStruct((positions, width), bf16),
+            jax.ShapeDtypeStruct((positions, channels), bf16),
+            jax.ShapeDtypeStruct((channels, positions), bf16),
+            jax.ShapeDtypeStruct((2, *tw.shape), bf16),
         ),
-        in_specs=[VMEM, VMEM, VMEM, ANY, ANY],
-        out_specs=(VMEM, VMEM, ANY, ANY),
+        in_specs=[ANY, ANY, ANY, ANY],
+        out_specs=(VMEM, VMEM, VMEM, VMEM, ANY),
         scratch_shapes=[
-            pltpu.VMEM((rows, width), jnp.bfloat16),
-            pltpu.VMEM((rows, width), jnp.bfloat16),
-            pltpu.VMEM(tw.shape, jnp.bfloat16),
-            DMA((2,)),
+            pltpu.VMEM(feat.shape, bf16),
+            pltpu.VMEM(w3.shape, bf16),
+            pltpu.VMEM(pw.shape, bf16),
+            pltpu.VMEM(tw.shape, bf16),
+            pltpu.VMEM(feat.shape, bf16),
+            pltpu.VMEM((positions, width), bf16),
+            pltpu.VMEM((positions, width), bf16),
+            pltpu.VMEM((positions, width), bf16),
+            pltpu.VMEM((positions, width), bf16),
+            pltpu.VMEM((positions, width), f32),
+            pltpu.VMEM((positions, width), bf16),
+            pltpu.VMEM(pw.shape, bf16),
+            DMA((5,)), DMA((2,)),
             DMA((2,)), DMA((2,)),
             DMA, DMA,
+            DMA((4,)), DMA((4,)),
             DMA((3,)), DMA((3,)),
-            DMA((3,)), DMA((3,)),
-            DMA((7,)), DMA((7,)),
-            DMA((7,)), DMA((7,)),
-            DMA((20,)), DMA((20,)),
+            DMA((4,)), DMA((4,)),
+            DMA((2, 3)), DMA((2, 3)),
+            DMA((17,)), DMA((17,)),
         ],
-        compiler_params=pltpu.CompilerParams(collective_id=0, has_side_effects=True),
+        compiler_params=pltpu.CompilerParams(
+            collective_id=0, has_side_effects=True, vmem_limit_bytes=67043328
+        ),
         name="forward_exchange",
-    )(q0, q2, centre, tw, pw)
-
-
-COLS = 256
-HALVES, PIECES = 2, 2
-
-
-def cols_at(start, size):
-    return pl.ds(pl.multiple_of(start, 128), size)
-
-
-def repeat(count, step, start=0):
-    def once(at, carry):
-        step(at)
-        return carry
-
-    lax.fori_loop(start, count, once, 0)
+    )(feat, w3, tw, pw)
 
 
 def backward_kernel(
-    feat, hidden, middle, act_t, tw, cot, pw, pwo, w3, grad_out, summed,
-    v_feat, v_act, v_tw, v_cot, v_pw, v_pwo, v_w3, block, score, out_grad, slope_f, slope_m,
+    feat, hidden, middle, block_hbm, act_hbm, tw, cot, pw, w3, grad_out, summed,
+    v_feat, block, act_t, v_tw, v_cot, v_pw, v_w3, score, out_grad, slope_f, slope_m,
     hid_grad, mid_grad, later, earlier, swap_out, swap_in, act_out, act_in,
     early, late, sib_early, sib_late, ring_out, ring_in, final, early_out, early_in,
     y_out, y_in, z_tile, z_out, z_in,
@@ -373,7 +422,7 @@
     loads = [
         pltpu.make_async_copy(source, target, load.at[slot])
         for slot, (source, target) in enumerate(
-            ((feat, v_feat), (pw, v_pw), (pwo, v_pwo), (cot, v_cot), (act_t, v_act), (w3, v_w3))
+            ((block_hbm, block), (cot, v_cot), (feat, v_feat), (pw, v_pw), (act_hbm, act_t), (w3, v_w3))
         )
     ]
     whole, tail = tracks // COLS, tracks % COLS
@@ -382,24 +431,13 @@
         where = cols_at(at * COLS, size)
         return pltpu.make_async_copy(tw.at[:, where], v_tw.at[:, where], tw_load.at[at])
 
-    for copy in loads[:3]:
-        copy.start()
+    loads[0].start()
     repeat(whole, lambda at: tw_copy(at).start())
     tw_copy(whole, tail).start()
-    for copy in loads[3:]:
+    for copy in loads[1:]:
         copy.start()
-    for copy in loads[:3]:
-        copy.wait()
-
-    def block_step(at):
-        cols, where = cols_at(at * COLS, COLS), rows_at(at * COLS, COLS)
-        value = v_feat[:, cols].astype(f32)
-        value = value + times_transposed(hidden[0], v_pw[where, :])
-        value = value + times_transposed(hidden[1], v_pwo[where, :])
-        block[:, cols] = value.astype(bf16)
-
-    repeat(chunks, block_step)
-    loads[3].wait()
+    loads[0].wait()
+    loads[1].wait()
 
     def score_step(at, size=COLS):
         tw_copy(at, size).wait()
@@ -419,6 +457,8 @@
         swap_copy(at).start()
 
     repeat(chunks, swap_step)
+    loads[2].wait()
+    loads[3].wait()
     slope_m[...] = gelu_slope(middle[...])
     hid_grad[...] = jnp.zeros_like(hid_grad)
 
@@ -435,7 +475,7 @@
         out_grad[at] = value
         rounded = value.astype(bf16)
         hid_grad[...] += times(rounded, v_pw[where, :])
-        early[0, where, :] = transposed_times(rounded, hidden[0]).astype(bf16)
+        early[0, where, :] = transposed_times(rounded, hidden[...]).astype(bf16)
 
     repeat(chunks, gather_step)
     mid_grad[...] = (hid_grad[...] * slope_m[...]).astype(bf16)
@@ -446,7 +486,7 @@
 
     def centre_step(at):
         where = rows_at(at * rows, rows)
-        early[1, where, :] = times(v_act[where, :], mid_grad[...]).astype(bf16)
+        early[1, where, :] = times(act_t[where, :], mid_grad[...]).astype(bf16)
 
     repeat(NZ, centre_step)
     order = (7, 1, 6, 2, 5, 3, 4, 0)
@@ -495,8 +535,8 @@
     def late_step(turn):
         at = lax.rem(z + turn, NZ)
         where = rows_at(at * rows, rows)
-        late[0, where, :] = times(v_act[where, :], later[...]).astype(bf16)
-        late[1, where, :] = times(v_act[where, :], earlier[...]).astype(bf16)
+        late[0, where, :] = times(act_t[where, :], later[...]).astype(bf16)
+        late[1, where, :] = times(act_t[where, :], earlier[...]).astype(bf16)
         late_sibling(at).start()
 
     def y_copy(at, step):
@@ -604,7 +644,7 @@
             ref = z_in.at[source, lax.rem(corner + 4 - twist, 4)]
             remote(ref, ref, z_s.at[turn - 1, twist], z_r.at[turn - 1, twist], z=z).wait_recv()
     for core in range(2):
-        total = jnp.zeros((each, hidden.shape[2]), f32)
+        total = jnp.zeros((each, hidden.shape[1]), f32)
         for turn in range(NZ):
             for sample in range(2):
                 total = total + z_in[turn, core * 2 + sample].astype(f32)
@@ -613,7 +653,7 @@
         ref = early_in.at[lax.rem(me + 16 - step, 16)]
         remote(ref, ref, fin_s.at[step - 1], fin_r.at[step - 1], z=z).wait_recv()
     for core in range(2):
-        total = jnp.zeros((each, hidden.shape[2]), f32)
+        total = jnp.zeros((each, hidden.shape[1]), f32)
         for row in range(NY):
             for sample in range(2):
                 total = total + early_in[(row * 2 + core) * 2 + sample].astype(f32)
@@ -645,7 +685,7 @@
         fin_copy(step).wait_send()
 
 
-def backward(feat, hidden, middle, act_t, tw, cot, pw, pwo, w3):
+def backward(feat, hidden, middle, block, act_t, tw, cot, pw, w3):
     bf16, f32 = jnp.bfloat16, jnp.float32
     positions, channels = feat.shape
     width = pw.shape[1]
@@ -667,13 +707,12 @@
         out_specs=(VMEM, VMEM),
         scratch_shapes=[
             pltpu.VMEM(feat.shape, bf16),
+            pltpu.VMEM(feat.shape, bf16),
             pltpu.VMEM(act_t.shape, bf16),
             pltpu.VMEM(tw.shape, bf16),
             pltpu.VMEM(cot.shape, bf16),
             pltpu.VMEM(pw.shape, bf16),
-            pltpu.VMEM(pwo.shape, bf16),
             pltpu.VMEM(w3.shape, bf16),
-            pltpu.VMEM((positions, channels), bf16),
             pltpu.VMEM((positions, tracks), bf16),
             pltpu.VMEM(tile, f32),
             pltpu.VMEM(tile, f32),
@@ -712,30 +751,24 @@
             DMA((NZ, 4)), DMA((NZ, 4)),
         ],
         compiler_params=pltpu.CompilerParams(
-            collective_id=1, has_side_effects=True, vmem_limit_bytes=60 * 1024 * 1024
+            collective_id=1, has_side_effects=True, vmem_limit_bytes=60000000
         ),
         name="backward",
-    )(feat, hidden, middle, act_t, tw, cot, pw, pwo, w3)
+    )(feat, hidden, middle, block, act_t, tw, cot, pw, w3)
 
 
 def body(features, dilated_weight, point_weight, track_weight, track_cotangent):
     samples, positions, channels = features.shape
     number_rows = samples * positions
-    width = dilated_weight.shape[2]
     feat = features.reshape(number_rows, channels)
-    activated = gelu_value(feat.astype(jnp.float32)).astype(jnp.bfloat16)
     taps_weight = jnp.transpose(dilated_weight, (1, 0, 2))
-    to_later = times(activated, taps_weight[0]).astype(jnp.bfloat16)
-    to_earlier = times(activated, taps_weight[2]).astype(jnp.bfloat16)
-    centre = times(activated, taps_weight[1])
-    middle, hidden, whole_track, other_point = forward_exchange(
-        to_later, to_earlier, centre, track_weight, point_weight
+    middle, hidden, block, turned, whole_track = forward_exchange(
+        feat, taps_weight, track_weight, point_weight
     )
     whole_track = whole_track.reshape(channels, track_weight.shape[1])
     cotangent = track_cotangent.reshape(number_rows, whole_track.shape[1])
     input_grad, summed = backward(
-        feat, hidden, middle, activated.T, whole_track, cotangent, point_weight, other_point,
-        taps_weight,
+        feat, hidden, middle, block, turned, whole_track, cotangent, point_weight, taps_weight
     )
     dilated_grad = jnp.stack([summed[2], summed[1], summed[3]], axis=1)
     return (input_grad.reshape(samples, positions, channels), dilated_grad, summed[0])

time: 127 us -> 117 us (0.921)
  matrix products: 5.93 us -> 0 us
  Pallas kernels: 114 us -> 112 us
  other arithmetic: 1.42 us -> 0.01 us
    dot_general x3 -> x0, matrix products: 5.93 us -> none  [times(): return jnp.dot(left, right, preferred_element_type=jnp.float32)]
    transpose x1 -> x0, other arithmetic: 1.42 us -> none  [body(): input_grad, summed = backward(feat, hidden, middle, activated.T, whole_tr...]
    unnamed x7 -> x2, local copies, waits for them, and re-layouts: 3.01 us -> 2.72 us
where the time goes in v3:
time: 117 us
  Pallas kernels  112 us (96%)
  local copies, waits for them, and re-layouts  4.13 us (4%)
    pallas_call x1, Pallas kernels, backward(): pl.pallas_call(backward_kernel, out_shape=(jax.ShapeDtypeStruct((position...  75.6 us
    pallas_call x1, Pallas kernels, forward_exchange(): pl.pallas_call(forward_kernel, out_shape=(jax.ShapeDtypeStruct((positions...  36.9 us
    unnamed x2, local copies, waits for them, and re-layouts  2.72 us

profile of v3, /device:TPU:1, one launch (start us, length us, event | category | flops | bytes accessed | tf_op | source)
XLA Modules:
  0.0 117.2 jit_solution(5603934519439052086)
XLA Ops:
  0.6 36.9 %forward_exchange.1 = (f32[256,384]{1,0:T(8,128)}, bf16[256,384]{1,0:T(8,128)(2,1)}, bf16[256,1536]{1,0:T(8,128)(2,1)}, bf16[1536,256]{1,0:T(8,128)(2,1)}, bf16[2,768,1920]{2,1,0:T(8,128)(2,1)}) custom-call(bf16[256,1536]{1,0:T(8,128)(2,1)} %bitcast.16, bf16[3,1536,384]{2,1,0:T(8,128)(2,1)} %bitcast.13, bf16[768,1920]{1,0:T(8,128)(2,1)} %tw.1, ...), custom_call_target="tpu_custom_call" | custom-call | tf_op jit(solution)/shard_map/forward_exchange/pallas_call | solution.py:346
  37.5 75.6 %backward.1 = (bf16[256,1536]{1,0:T(8,128)(2,1)}, f32[4,12,384]{2,1,0:T(8,128)}) custom-call(bf16[256,1536]{1,0:T(8,128)(2,1)} %bitcast.17, bf16[256,384]{1,0:T(8,128)(2,1)} %get-tuple-element.10.hidden, f32[256,384]{1,0:T(8,128)} %get-tuple-element.11.middle, bf16[256,1536]{1,0:T(8,128)(2,1)} %get-tuple-element.12.block_hbm, ...), custom_call_target="tpu_custom_call" | custom-call | tf_op jit(solution)/shard_map/backward/pallas_call | solution.py:700
  113.1 1.4 %slice_bitcast_fusion = (f32[12,384]{1,0:T(8,128)}, f32[12,1,384]{2,0,1:T(8,128)S(1)}, f32[12,1,384]{2,0,1:T(8,128)S(1)}, f32[12,1,384]{2,0,1:T(8,128)S(1)}) fusion(f32[4,12,384]{2,1,0:T(8,128)} %get-tuple-element.16), kind=kLoop, calls=%fused_computation.1 | loop fusion | bytes 147456 | tf_op jit(solution)/shard_map/squeeze | solution.py:774
  114.5 0.7 copy.8
  115.1 2.1 %copy.10 = bf16[1,256,1536]{2,1,0:T(8,128)(2,1)} copy(bf16[1,256,1536]{2,1,0:T(8,128)(2,1)} %bitcast.19) | data formatting | bytes 1572864
  (1 shorter events, 0.0 us)

commit v4 on v3

--- a/solution.py
+++ b/solution.py
@@ -553,16 +553,6 @@
         for step in range(1, NY):
             y_copy(at, step).start()
 
-    def late_and_y_step(turn):
-        late_step(turn)
-        y_step(turn - 1)
-
-    late_step(1)
-    repeat(NZ + 1, late_and_y_step, 2)
-    y_step(NZ)
-    ring_step(3)
-    loads[5].wait()
-
     def act_copy(at):
         return remote(act_out.at[at], act_in.at[at], acts_s.at[at], acts_r.at[at], h=1 - h)
 
@@ -574,8 +564,20 @@
         act_out[at] = value.astype(bf16)
         act_copy(at).start()
 
-    repeat(chunks, act_step)
+    def mixed_step(turn):
+        act_step(turn - 1)
+        late_step(turn + 1)
+        y_step(turn)
+
+    loads[5].wait()
+    late_step(1)
+    repeat(chunks // 2 + 1, mixed_step, 1)
+    ring_step(3)
+    repeat(chunks + 1, mixed_step, chunks // 2 + 1)
     ring_step(4)
+    late_step(NZ)
+    y_step(NZ - 1)
+    y_step(NZ)
 
     def z_copy(turn, at, twist):
         to = lax.rem(corner + twist, 4)

time: 117 us -> 113 us (0.966)
  Pallas kernels: 112 us -> 108 us
    pallas_call x1, Pallas kernels: 75.6 us -> 71.6 us  [backward(): pl.pallas_call(backward_kernel, out_shape=(jax.ShapeDtypeStruct((position...]
where the time goes in v4:
time: 113 us
  Pallas kernels  108 us (96%)
  local copies, waits for them, and re-layouts  4.13 us (4%)
    pallas_call x1, Pallas kernels, backward(): pl.pallas_call(backward_kernel, out_shape=(jax.ShapeDtypeStruct((position...  71.6 us
    pallas_call x1, Pallas kernels, forward_exchange(): pl.pallas_call(forward_kernel, out_shape=(jax.ShapeDtypeStruct((positions...  36.9 us
    unnamed x2, local copies, waits for them, and re-layouts  2.72 us

profile of v4, /device:TPU:1, one launch (start us, length us, event | category | flops | bytes accessed | tf_op | source)
XLA Modules:
  0.0 113.2 jit_solution(13729658861595205595)
XLA Ops:
  0.6 36.9 %forward_exchange.1 = (f32[256,384]{1,0:T(8,128)}, bf16[256,384]{1,0:T(8,128)(2,1)}, bf16[256,1536]{1,0:T(8,128)(2,1)}, bf16[1536,256]{1,0:T(8,128)(2,1)}, bf16[2,768,1920]{2,1,0:T(8,128)(2,1)}) custom-call(bf16[256,1536]{1,0:T(8,128)(2,1)} %bitcast.16, bf16[3,1536,384]{2,1,0:T(8,128)(2,1)} %bitcast.13, bf16[768,1920]{1,0:T(8,128)(2,1)} %tw.1, ...), custom_call_target="tpu_custom_call" | custom-call | tf_op jit(solution)/shard_map/forward_exchange/pallas_call | solution.py:346
  37.5 71.6 %backward.1 = (bf16[256,1536]{1,0:T(8,128)(2,1)}, f32[4,12,384]{2,1,0:T(8,128)}) custom-call(bf16[256,1536]{1,0:T(8,128)(2,1)} %bitcast.17, bf16[256,384]{1,0:T(8,128)(2,1)} %get-tuple-element.10.hidden, f32[256,384]{1,0:T(8,128)} %get-tuple-element.11.middle, bf16[256,1536]{1,0:T(8,128)(2,1)} %get-tuple-element.12.block_hbm, ...), custom_call_target="tpu_custom_call" | custom-call | tf_op jit(solution)/shard_map/backward/pallas_call | solution.py:702
  109.1 1.4 %slice_bitcast_fusion = (f32[12,384]{1,0:T(8,128)}, f32[12,1,384]{2,0,1:T(8,128)S(1)}, f32[12,1,384]{2,0,1:T(8,128)S(1)}, f32[12,1,384]{2,0,1:T(8,128)S(1)}) fusion(f32[4,12,384]{2,1,0:T(8,128)} %get-tuple-element.16), kind=kLoop, calls=%fused_computation.1 | loop fusion | bytes 147456 | tf_op jit(solution)/shard_map/squeeze | solution.py:776
  110.5 0.7 copy.8
  111.2 2.1 %copy.10 = bf16[1,256,1536]{2,1,0:T(8,128)(2,1)} copy(bf16[1,256,1536]{2,1,0:T(8,128)(2,1)} %bitcast.19) | data formatting | bytes 1572864
  (1 shorter events, 0.0 us)

commit v5 on v4

--- a/solution.py
+++ b/solution.py
@@ -155,8 +155,8 @@
 
 
 def forward_kernel(
-    feat, w3, tw, pw, middle, hid_own, block, act_t, twf,
-    v_feat, v_w3, v_pw, own, act, ahead_out, behind_out, from_before, from_after, centre, hid_other, pwo,
+    feat, w3, tw, pw, mid_hbm, hid_hbm, block, act_hbm, twf,
+    middle, hid_own, act_t, v_feat, v_w3, v_pw, own, act, ahead_out, behind_out, from_before, from_after, centre, hid_other, pwo,
     load, own_sem, halo_s, halo_r, hid_s, hid_r, x_s, x_r, y_s, y_r, pz_s, pz_r, tz_s, tz_r, sib_s, sib_r,
 ):
     z, y, c, h, s = place()
@@ -277,6 +277,11 @@
         act_t[rows_at(at * COLS, COLS), :] = act[:, cols_at(at * COLS, COLS)].T
 
     repeat(chunks, turn_step)
+    stores = [
+        pltpu.make_async_copy(source, target, load.at[5 + slot])
+        for slot, (source, target) in enumerate(((act_t, act_hbm), (middle, mid_hbm), (hid_own, hid_hbm)))
+    ]
+    stores[0].start()
 
     def p_from(core, slot):
         at = z + NZ - steps[slot]
@@ -299,18 +304,17 @@
     middle[...] = total
     hid_own[...] = gelu_value(total).astype(bf16)
     go(hid_own, hid_other, hid_s, hid_r, h=1 - h)
-
-    for cut in range(2):
+    stores[1].start()
+    stores[2].start()
+
+    def take_z(cut):
         for slot in range(3):
             here = t_from(c, cut, slot)
             landing(here, tz_s.at[cut, slot], tz_r.at[cut, slot])
             at = 7 + cut * 3 + slot
             go(here, here, sib_s.at[at], sib_r.at[at], c=1 - c)
-    for step in range(1, NY):
-        here = y_from(c, step)
-        landing(here, y_s.at[step - 1], y_r.at[step - 1])
-        go(here, here, sib_s.at[13 + step], sib_r.at[13 + step], c=1 - c)
-
+
+    take_z(0)
     landing(pwo.at[p_rows_of(1 - c, z, None)], sib_s.at[0], sib_r.at[0])
     for slot in range(4):
         landing(p_from(1 - c, slot), sib_s.at[1 + slot], sib_r.at[1 + slot])
@@ -325,6 +329,12 @@
         block[:, cols] = value.astype(bf16)
 
     repeat(chunks, block_step)
+    take_z(1)
+    for step in range(1, NY):
+        here = y_from(c, step)
+        landing(here, y_s.at[step - 1], y_r.at[step - 1])
+        go(here, here, sib_s.at[13 + step], sib_r.at[13 + step], c=1 - c)
+
     for cut in range(2):
         landing(twf.at[other, z_rows(1 - c, z, cut)], sib_s.at[5 + cut], sib_r.at[5 + cut])
         for slot in range(3):
@@ -337,6 +347,8 @@
         copy.wait_send()
     drain_halo(z, y, ahead, behind, halo_s, halo_r)
     put_own.wait()
+    for copy in stores:
+        copy.wait()
 
 
 def forward_exchange(feat, w3, tw, pw):
@@ -353,8 +365,11 @@
             jax.ShapeDtypeStruct((2, *tw.shape), bf16),
         ),
         in_specs=[ANY, ANY, ANY, ANY],
-        out_specs=(VMEM, VMEM, VMEM, VMEM, ANY),
+        out_specs=(ANY, ANY, VMEM, ANY, ANY),
         scratch_shapes=[
+            pltpu.VMEM((positions, width), f32),
+            pltpu.VMEM((positions, width), bf16),
+            pltpu.VMEM((channels, positions), bf16),
             pltpu.VMEM(feat.shape, bf16),
             pltpu.VMEM(w3.shape, bf16),
             pltpu.VMEM(pw.shape, bf16),
@@ -367,7 +382,7 @@
             pltpu.VMEM((positions, width), f32),
             pltpu.VMEM((positions, width), bf16),
             pltpu.VMEM(pw.shape, bf16),
-            DMA((5,)), DMA((2,)),
+            DMA((8,)), DMA((2,)),
             DMA((2,)), DMA((2,)),
             DMA, DMA,
             DMA((4,)), DMA((4,)),
@@ -384,8 +399,8 @@
 
 
 def backward_kernel(
-    feat, hidden, middle, block_hbm, act_hbm, tw, cot, pw, w3, grad_out, summed,
-    v_feat, block, act_t, v_tw, v_cot, v_pw, v_w3, score, out_grad, slope_f, slope_m,
+    feat, hid_hbm, mid_hbm, block_hbm, act_hbm, tw, cot, pw, w3, grad_out, summed,
+    hidden, middle, v_feat, block, act_t, v_tw, v_cot, v_pw, v_w3, score, out_grad, slope_f, slope_m,
     hid_grad, mid_grad, later, earlier, swap_out, swap_in, act_out, act_in,
     early, late, sib_early, sib_late, ring_out, ring_in, final, early_out, early_in,
     y_out, y_in, z_tile, z_out, z_in,
@@ -422,7 +437,7 @@
     loads = [
         pltpu.make_async_copy(source, target, load.at[slot])
         for slot, (source, target) in enumerate(
-            ((block_hbm, block), (cot, v_cot), (feat, v_feat), (pw, v_pw), (act_hbm, act_t), (w3, v_w3))
+            ((block_hbm, block), (cot, v_cot), (feat, v_feat), (pw, v_pw), (act_hbm, act_t), (w3, v_w3), (hid_hbm, hidden), (mid_hbm, middle))
         )
     ]
     whole, tail = tracks // COLS, tracks % COLS
@@ -432,10 +447,9 @@
         return pltpu.make_async_copy(tw.at[:, where], v_tw.at[:, where], tw_load.at[at])
 
     loads[0].start()
+    loads[1].start()
     repeat(whole, lambda at: tw_copy(at).start())
     tw_copy(whole, tail).start()
-    for copy in loads[1:]:
-        copy.start()
     loads[0].wait()
     loads[1].wait()
 
@@ -447,6 +461,8 @@
 
     repeat(whole, score_step)
     score_step(whole, tail)
+    for copy in loads[2:]:
+        copy.start()
     pl.semaphore_wait(barrier, greeted)
 
     def swap_copy(at):
@@ -457,8 +473,8 @@
         swap_copy(at).start()
 
     repeat(chunks, swap_step)
-    loads[2].wait()
-    loads[3].wait()
+    for slot in (2, 3, 6, 7):
+        loads[slot].wait()
     slope_m[...] = gelu_slope(middle[...])
     hid_grad[...] = jnp.zeros_like(hid_grad)
 
@@ -705,9 +721,11 @@
             jax.ShapeDtypeStruct((positions, channels), bf16),
             jax.ShapeDtypeStruct((4, each, width), f32),
         ),
-        in_specs=[ANY, VMEM, VMEM, ANY, ANY, ANY, ANY, ANY, ANY],
+        in_specs=[ANY] * 9,
         out_specs=(VMEM, VMEM),
         scratch_shapes=[
+            pltpu.VMEM(hidden.shape, bf16),
+            pltpu.VMEM(middle.shape, f32),
             pltpu.VMEM(feat.shape, bf16),
             pltpu.VMEM(feat.shape, bf16),
             pltpu.VMEM(act_t.shape, bf16),
@@ -741,7 +759,7 @@
             pltpu.VMEM((part, width), f32),
             pltpu.VMEM((NZ, 4, each, width), bf16),
             pltpu.VMEM((NZ, 4, each, width), bf16),
-            DMA((6,)), DMA((tracks // COLS + 1,)),
+            DMA((8,)), DMA((tracks // COLS + 1,)),
             DMA((chunks,)), DMA((chunks,)),
             DMA((chunks,)), DMA((chunks,)),
             DMA((2,)), DMA((2,)),

time: 113 us -> 112 us (level)
    pallas_call x1, Pallas kernels: 71.6 us -> 69.7 us  [backward(): pl.pallas_call(backward_kernel, out_shape=(jax.ShapeDtypeStruct((position...]
where the time goes in v5:
time: 112 us
  Pallas kernels  107 us (96%)
  local copies, waits for them, and re-layouts  4.13 us (4%)
    pallas_call x1, Pallas kernels, backward(): pl.pallas_call(backward_kernel, out_shape=(jax.ShapeDtypeStruct((position...  69.7 us
    pallas_call x1, Pallas kernels, forward_exchange(): pl.pallas_call(forward_kernel, out_shape=(jax.ShapeDtypeStruct((positions...  37.5 us
    unnamed x2, local copies, waits for them, and re-layouts  2.72 us

profile of v5, /device:TPU:1, one launch (start us, length us, event | category | flops | bytes accessed | tf_op | source)
XLA Modules:
  0.0 112.0 jit_solution(3631609156446752412)
XLA Ops:
  0.6 37.5 %forward_exchange.1 = (f32[256,384]{1,0:T(8,128)}, bf16[256,384]{1,0:T(8,128)(2,1)}, bf16[256,1536]{1,0:T(8,128)(2,1)}, bf16[1536,256]{1,0:T(8,128)(2,1)}, bf16[2,768,1920]{2,1,0:T(8,128)(2,1)}) custom-call(bf16[256,1536]{1,0:T(8,128)(2,1)} %bitcast.16, bf16[3,1536,384]{2,1,0:T(8,128)(2,1)} %bitcast.13, bf16[768,1920]{1,0:T(8,128)(2,1)} %tw.1, ...), custom_call_target="tpu_custom_call" | custom-call | tf_op jit(solution)/shard_map/forward_exchange/pallas_call | solution.py:358
  38.2 69.7 %backward.1 = (bf16[256,1536]{1,0:T(8,128)(2,1)}, f32[4,12,384]{2,1,0:T(8,128)}) custom-call(bf16[256,1536]{1,0:T(8,128)(2,1)} %bitcast.17, bf16[256,384]{1,0:T(8,128)(2,1)} %get-tuple-element.10.hid_hbm, f32[256,384]{1,0:T(8,128)} %get-tuple-element.11.mid_hbm, bf16[256,1536]{1,0:T(8,128)(2,1)} %get-tuple-element.12.block_hbm, ...), custom_call_target="tpu_custom_call" | custom-call | tf_op jit(solution)/shard_map/backward/pallas_call | solution.py:718
  107.9 1.4 %slice_bitcast_fusion = (f32[12,384]{1,0:T(8,128)}, f32[12,1,384]{2,0,1:T(8,128)S(1)}, f32[12,1,384]{2,0,1:T(8,128)S(1)}, f32[12,1,384]{2,0,1:T(8,128)S(1)}) fusion(f32[4,12,384]{2,1,0:T(8,128)} %get-tuple-element.16), kind=kLoop, calls=%fused_computation.1 | loop fusion | bytes 147456 | tf_op jit(solution)/shard_map/squeeze | solution.py:794
  109.3 0.7 copy.8
  109.9 2.1 %copy.10 = bf16[1,256,1536]{2,1,0:T(8,128)(2,1)} copy(bf16[1,256,1536]{2,1,0:T(8,128)(2,1)} %bitcast.19) | data formatting | bytes 1572864
  (1 shorter events, 0.0 us)

commit v6 on v5

--- a/solution.py
+++ b/solution.py
@@ -178,10 +178,8 @@
             ((feat, v_feat), (w3.at[0], v_w3.at[0]), (w3.at[2], v_w3.at[2]), (w3.at[1], v_w3.at[1]), (pw, v_pw))
         )
     ]
-    for copy in loads:
+    for copy in loads[:3]:
         copy.start()
-    take_own = pltpu.make_async_copy(tw, own, own_sem.at[0])
-    take_own.start()
 
     half = tw.shape[0] // 2
     point = pw.shape[0] // 2
@@ -246,6 +244,10 @@
     def _():
         remote(*behind, halo_s.at[1], halo_r.at[1], **shifted(z, y, -2)).start()
 
+    for copy in loads[3:]:
+        copy.start()
+    take_own = pltpu.make_async_copy(tw, own, own_sem.at[0])
+    take_own.start()
     steps = (1, NZ - 1, 2, NZ - 2)
     here = pwo.at[p_rows_of(c, z, None)]
     landing(here, x_s.at[0], x_r.at[0])

time: 112 us -> 112 us (level)
  no operation moved by 1% of the time
where the time goes in v6:
time: 112 us
  Pallas kernels  107 us (96%)
  local copies, waits for them, and re-layouts  4.13 us (4%)
    pallas_call x1, Pallas kernels, backward(): pl.pallas_call(backward_kernel, out_shape=(jax.ShapeDtypeStruct((position...  69.7 us
    pallas_call x1, Pallas kernels, forward_exchange(): pl.pallas_call(forward_kernel, out_shape=(jax.ShapeDtypeStruct((positions...  37.5 us
    unnamed x2, local copies, waits for them, and re-layouts  2.72 us

profile of v6, /device:TPU:1, one launch (start us, length us, event | category | flops | bytes accessed | tf_op | source)
XLA Modules:
  0.0 112.0 jit_solution(5302526892226249336)
XLA Ops:
  0.6 37.5 %forward_exchange.1 = (f32[256,384]{1,0:T(8,128)}, bf16[256,384]{1,0:T(8,128)(2,1)}, bf16[256,1536]{1,0:T(8,128)(2,1)}, bf16[1536,256]{1,0:T(8,128)(2,1)}, bf16[2,768,1920]{2,1,0:T(8,128)(2,1)}) custom-call(bf16[256,1536]{1,0:T(8,128)(2,1)} %bitcast.16, bf16[3,1536,384]{2,1,0:T(8,128)(2,1)} %bitcast.13, bf16[768,1920]{1,0:T(8,128)(2,1)} %tw.1, ...), custom_call_target="tpu_custom_call" | custom-call | tf_op jit(solution)/shard_map/forward_exchange/pallas_call | solution.py:360
  38.2 69.7 %backward.1 = (bf16[256,1536]{1,0:T(8,128)(2,1)}, f32[4,12,384]{2,1,0:T(8,128)}) custom-call(bf16[256,1536]{1,0:T(8,128)(2,1)} %bitcast.17, bf16[256,384]{1,0:T(8,128)(2,1)} %get-tuple-element.10.hid_hbm, f32[256,384]{1,0:T(8,128)} %get-tuple-element.11.mid_hbm, bf16[256,1536]{1,0:T(8,128)(2,1)} %get-tuple-element.12.block_hbm, ...), custom_call_target="tpu_custom_call" | custom-call | tf_op jit(solution)/shard_map/backward/pallas_call | solution.py:720
  107.9 1.4 %slice_bitcast_fusion = (f32[12,384]{1,0:T(8,128)}, f32[12,1,384]{2,0,1:T(8,128)S(1)}, f32[12,1,384]{2,0,1:T(8,128)S(1)}, f32[12,1,384]{2,0,1:T(8,128)S(1)}) fusion(f32[4,12,384]{2,1,0:T(8,128)} %get-tuple-element.16), kind=kLoop, calls=%fused_computation.1 | loop fusion | bytes 147456 | tf_op jit(solution)/shard_map/squeeze | solution.py:796
  109.3 0.7 copy.8
  110.0 2.1 %copy.10 = bf16[1,256,1536]{2,1,0:T(8,128)(2,1)} copy(bf16[1,256,1536]{2,1,0:T(8,128)(2,1)} %bitcast.19) | data formatting | bytes 1572864
  (1 shorter events, 0.0 us)
